TPU v7x, 32 devices: a whole 2x2x4 slice. The times are simulated.
32 devices in a mesh: tok: 4 (over z), row: 4 (over y, x), col: 2 (over core).
Axes of the slice: x: 2, y: 2, z: 4, core: 2. Of those that a mesh axis runs over, the one named last changes fastest.
Arguments:
- hidden_in: bfloat16 [4096, 2048], P(('tok', 'row', 'col')), may hold values from -6 to 6
- seg_ids: int32 [16, 256], P(('tok', 'row')), may hold values from 0 to 3, never falling along the last dimension, each value on 1 to 128 neighbouring positions
- expert_ids: int32 [4096, 8], P(('tok', 'row', 'col')), may hold values from 0 to 31, all different within a row; in each aligned block of 128 rows (0 to 127, 128 to 255, ...) at most 64 rows name the same one
- norm1_gain: float32 [2048], replicated, may hold values from 0.5 to 1.5
- query_gain: float32 [128], replicated, may hold values from 0.5 to 1.5
- key_gain: float32 [128], replicated, may hold values from 0.5 to 1.5
- w_query: bfloat16 [2048, 4096], P('row', 'col'), may hold values from -0.125 to 0.125
- w_keyval: bfloat16 [2048, 1024], P('row', 'col'), may hold values from -0.125 to 0.125
- w_output: bfloat16 [4096, 2048], P('col', 'row'), may hold values from -0.75 to 0.75
- norm2_gain: float32 [2048], replicated, may hold values from 0.5 to 1.5
- router: bfloat16 [2048, 32], replicated, may hold values from -0.0625 to 0.0625
- w_gate_up: bfloat16 [32, 2048, 1536], P(('tok', 'row', 'col')), may hold values from -0.125 to 0.125
- w_down: bfloat16 [32, 768, 2048], P(('tok', 'row', 'col')), may hold values from -0.875 to 0.875
- cotangent: bfloat16 [4096, 2048], P(('tok', 'row', 'col')), may hold values from -6 to 6
Outputs:
- layer_out: bfloat16 [4096, 2048], P(('tok', 'row', 'col'))
- input_grad: bfloat16 [4096, 2048], P(('tok', 'row', 'col'))
- w_query_grad: float32 [2048, 4096], P('row', 'col')
- w_keyval_grad: float32 [2048, 1024], P('row', 'col')
- w_output_grad: float32 [4096, 2048], P('col', 'row')
- router_grad: float32 [2048, 32], replicated
- gate_up_grad: float32 [32, 2048, 1536], P(('tok', 'row', 'col'))
- down_grad: float32 [32, 768, 2048], P(('tok', 'row', 'col'))
- norm1_grad: float32 [2048], replicated
- norm2_grad: float32 [2048], replicated
- query_gain_grad: float32 [128], replicated
- key_gain_grad: float32 [128], replicated
Inputs may be any that keep to these rules, and one draw needn't show every extreme that they name: `seg_ids`: in each row the values never fall; each sequence has 1 to 128 tokens, and one has exactly 128. `expert_ids`: each row names 8 different experts; in the rows of one device (aligned blocks of 128 rows) no expert is named by more than 64 rows, a bound that some block reaches.
All inputs are finite; a program needn't handle non-finite values.
Results may differ from a plain program's by a relative error of at most 0.023.
Values may be sent and summed in bfloat16 or wider, within the bound.
No kernel may reach another device: no remote copies, remote signals or barrier semaphores. Data moves between devices by JAX's collectives and lax.ppermute only.
A program may use at most 256 MiB of HBM per device.

v0:
```python
import functools
import math

import jax
import jax.numpy as jnp
from jax import lax
from jax.experimental import pallas as pl
from jax.experimental.pallas import tpu as pltpu
from jax.sharding import PartitionSpec as P


D = 2048
HQ = 32
KV = 4
HD = 128
FF = 768
TOPK = 8
EPSILON = 1e-06
ROPE_BASE = 1000000.0
BF = jnp.bfloat16
F32 = jnp.float32
ALL = ("tok", "row", "col")


def matmul(left, right):
    return jnp.dot(left, right, preferred_element_type=F32)


def contract(left, right, dims):
    return lax.dot_general(left, right, (dims, ((), ())), preferred_element_type=F32)


def rms_scale(values, gain):
    return values * lax.rsqrt(jnp.mean(values * values, axis=-1, keepdims=True) + EPSILON) * gain


def total(*parts):
    acc = parts[0].astype(F32)
    for part in parts[1:]:
        acc = acc + part.astype(F32)
    return acc


def flip(values, axis, mask, size):
    return lax.ppermute(values, axis, [(i, i ^ mask) for i in range(size)])


def estimate(flops, *arrays):
    moved = sum(math.prod(x.shape) * x.dtype.itemsize for x in arrays)
    return pl.CostEstimate(flops=flops, bytes_accessed=moved, transcendentals=0)


def turn(rows, cos_ref, sin_ref):
    return rows * cos_ref[0] + pltpu.roll(rows, HD // 2, 1) * sin_ref[0]


def turn_back(rows, cos_ref, sin_ref):
    return rows * cos_ref[0] + pltpu.roll(rows * sin_ref[0], HD // 2, 1)


def inverse_rms(rows):
    return lax.rsqrt(jnp.mean(rows * rows, axis=-1, keepdims=True) + EPSILON)


def head_of(ref, head):
    part = ref[:, 0, :, head * HD : (head + 1) * HD]
    return part.reshape(part.shape[0] * part.shape[1], HD)


def put_head(ref, head, rows):
    shape = ref.shape
    ref[:, 0, :, head * HD : (head + 1) * HD] = rows.reshape(shape[0], shape[2], HD).astype(
        ref.dtype
    )


def softmax_of(query_rows, key_rows, mask_ref):
    scores = contract(query_rows, key_rows, ((1,), (1,))) * (1.0 / math.sqrt(HD))
    raised = jnp.where(mask_ref[0] > 0.0, jnp.exp(scores), 0.0)
    return raised / jnp.sum(raised, axis=-1, keepdims=True)


def key_parts(heads, raw_ref):
    key_raw = head_of(raw_ref, heads).astype(BF).astype(F32)
    value_rows = head_of(raw_ref, heads + 1).astype(BF)
    return key_raw, value_rows


def attend_kernel(heads, raw_ref, cos_ref, sin_ref, mask_ref, qg_ref, kg_ref, out_ref):
    key_raw, value_rows = key_parts(heads, raw_ref)
    key_rows = turn(key_raw * inverse_rms(key_raw) * kg_ref[...], cos_ref, sin_ref).astype(BF)
    for head in range(heads):
        raw = head_of(raw_ref, head)
        query_rows = turn(raw * inverse_rms(raw) * qg_ref[...], cos_ref, sin_ref).astype(BF)
        attention = softmax_of(query_rows, key_rows, mask_ref).astype(BF)
        put_head(out_ref, head, contract(attention, value_rows, ((1,), (0,))))


def rms_back(raw, inverse, gain, grad):
    scaled = grad * gain
    inner = jnp.sum(scaled * raw, axis=-1, keepdims=True) * (1.0 / HD)
    raw_grad = inverse * scaled - raw * (inverse * inverse * inverse * inner)
    return raw_grad, jnp.sum(grad * raw * inverse, axis=0, keepdims=True)


def attend_back_kernel(
    heads,
    raw_ref,
    cos_ref,
    sin_ref,
    mask_ref,
    qg_ref,
    kg_ref,
    mixed_ref,
    grad_ref,
    send_ref,
    qgain_ref,
    kgain_ref,
):
    scale = 1.0 / math.sqrt(HD)
    key_raw, value_rows = key_parts(heads, raw_ref)
    key_inverse = inverse_rms(key_raw)
    key_rows = turn(key_raw * key_inverse * kg_ref[...], cos_ref, sin_ref).astype(BF)
    key_back = jnp.zeros(key_raw.shape, F32)
    value_back = jnp.zeros(key_raw.shape, F32)
    gain_sum = jnp.zeros((1, HD), F32)
    for head in range(heads):
        raw = head_of(raw_ref, head)
        inverse = inverse_rms(raw)
        query_rows = turn(raw * inverse * qg_ref[...], cos_ref, sin_ref).astype(BF)
        weights = softmax_of(query_rows, key_rows, mask_ref)
        grad = head_of(grad_ref, head)
        mixed = head_of(mixed_ref, head)
        value_back = value_back + contract(weights.astype(BF), grad, ((0,), (0,)))
        weight_grad = contract(grad, value_rows, ((1,), (1,)))
        delta = jnp.sum(grad.astype(F32) * mixed.astype(F32), axis=-1, keepdims=True)
        score_grad = (weights * (weight_grad - delta)).astype(BF)
        query_back = contract(score_grad, key_rows, ((1,), (0,))) * scale
        key_back = key_back + contract(score_grad, query_rows, ((0,), (0,))) * scale
        raw_grad, gain_part = rms_back(
            raw, inverse, qg_ref[...], turn_back(query_back, cos_ref, sin_ref)
        )
        gain_sum = gain_sum + gain_part
        put_head(send_ref, head, raw_grad)
    key_grad, kgain_part = rms_back(
        key_raw, key_inverse, kg_ref[...], turn_back(key_back, cos_ref, sin_ref)
    )
    put_head(send_ref, heads, key_grad)
    put_head(send_ref, heads + 1, value_back)

    @pl.when(pl.program_id(0) == 0)
    def _():
        qgain_ref[...] = jnp.zeros_like(qgain_ref)
        kgain_ref[...] = jnp.zeros_like(kgain_ref)

    qgain_ref[...] += gain_sum
    kgain_ref[...] += kgain_part


def group_spec(shape):
    return pl.BlockSpec((shape[0], 1) + shape[2:], lambda g: (0, g, 0, 0))


def table_spec(shape):
    return pl.BlockSpec((1,) + shape[1:], lambda g: (g, 0, 0))


def whole_spec(shape):
    return pl.BlockSpec(shape, lambda g: (0,) * len(shape))


def attention_specs(raw, cosine, sine, mask):
    return [
        group_spec(raw.shape),
        table_spec(cosine.shape),
        table_spec(sine.shape),
        table_spec(mask.shape),
        whole_spec((1, HD)),
        whole_spec((1, HD)),
    ]


def attend(heads, raw, cosine, sine, mask, qg, kg):
    shape = raw.shape[:3] + (heads * HD,)
    return pl.pallas_call(
        functools.partial(attend_kernel, heads),
        grid=(raw.shape[1],),
        in_specs=attention_specs(raw, cosine, sine, mask),
        out_specs=group_spec(shape),
        out_shape=jax.ShapeDtypeStruct(shape, BF),
        compiler_params=pltpu.CompilerParams(vmem_limit_bytes=56 << 20),
        cost_estimate=estimate(4 << 30, raw, mask),
        name="attend",
    )(raw, cosine, sine, mask, qg, kg)


def attend_back(heads, raw, cosine, sine, mask, qg, kg, mixed, grad):
    return pl.pallas_call(
        functools.partial(attend_back_kernel, heads),
        grid=(raw.shape[1],),
        in_specs=attention_specs(raw, cosine, sine, mask)
        + [group_spec(mixed.shape), group_spec(grad.shape)],
        out_specs=[
            group_spec(raw.shape),
            whole_spec((1, HD)),
            whole_spec((1, HD)),
        ],
        out_shape=[
            jax.ShapeDtypeStruct(raw.shape, BF),
            jax.ShapeDtypeStruct((1, HD), F32),
            jax.ShapeDtypeStruct((1, HD), F32),
        ],
        compiler_params=pltpu.CompilerParams(vmem_limit_bytes=56 << 20),
        cost_estimate=estimate(6 << 30, raw, raw, mask),
        name="attend_back",
    )(raw, cosine, sine, mask, qg, kg, mixed, grad)


def pick_kernel(counts, experts, capacity, scaled, *refs):
    pieces = refs[: len(counts)]
    rank_ref = refs[len(counts)]
    weight_ref = refs[len(counts) + 1] if scaled else None
    outs = refs[len(counts) + 1 + scaled : -2]
    select_ref, level_ref = refs[-2:]
    blocks, rows = rank_ref.shape[0], rank_ref.shape[2]
    places = [(p, i * rows) for p, count in enumerate(counts) for i in range(count)]
    slots = lax.broadcasted_iota(jnp.int32, (capacity, rows), 0).astype(F32)
    for block in range(blocks):
        for e in range(experts):
            hit = (slots == rank_ref[block, e : e + 1, :]).astype(F32)
            span = slice(e * capacity, (e + 1) * capacity)
            select_ref[block, span, :] = hit.astype(BF)
            if scaled:
                level = jnp.sum(hit * weight_ref[block, e : e + 1, :], axis=1, keepdims=True)
                level_ref[block, span, :] = jnp.broadcast_to(level, (capacity, 128))
    chunk = 256

    def body(step, carry):
        cols = pl.ds(pl.multiple_of(step * chunk, chunk), chunk)
        for block, (p, start) in enumerate(places):
            picked = matmul(select_ref[block], pieces[p][start : start + rows, cols])
            if scaled:
                picked = picked * jnp.concatenate([level_ref[block]] * (chunk // 128), axis=1)
            picked = picked.astype(BF)
            for e in range(experts):
                outs[e][block * capacity : (block + 1) * capacity, cols] = picked[
                    e * capacity : (e + 1) * capacity
                ]
        return carry

    lax.fori_loop(0, pieces[0].shape[1] // chunk, body, 0)


def pick(pieces, rank, capacity, weight=None):
    blocks, experts, rows = rank.shape
    operands = list(pieces) + [rank] + ([] if weight is None else [weight])
    counts = [piece.shape[0] // rows for piece in pieces]
    shape = jax.ShapeDtypeStruct((blocks * capacity, pieces[0].shape[1]), BF)
    return pl.pallas_call(
        functools.partial(pick_kernel, counts, experts, capacity, int(weight is not None)),
        in_specs=[pl.BlockSpec(memory_space=pltpu.VMEM)] * len(operands),
        out_specs=[pl.BlockSpec(memory_space=pltpu.VMEM)] * experts,
        out_shape=[shape] * experts,
        scratch_shapes=[
            pltpu.VMEM((blocks, experts * capacity, rows), BF),
            pltpu.VMEM((blocks, experts * capacity, 128), F32),
        ],
        compiler_params=pltpu.CompilerParams(vmem_limit_bytes=48 << 20),
        cost_estimate=estimate(1 << 30, *operands, *operands),
    )(*operands)


def spread_kernel(experts, capacity, scaled, *refs):
    rows_refs = refs[:experts]
    rank_ref = refs[experts]
    weight_ref = refs[experts + 1] if scaled else None
    outs = refs[experts + 1 + scaled : -2]
    place_ref, level_ref = refs[-2:]
    blocks, tokens = rank_ref.shape[0], rank_ref.shape[1]
    slots = lax.broadcasted_iota(jnp.int32, (tokens, capacity), 1).astype(F32)
    for block in range(blocks):
        for e in range(experts):
            hit = (slots == rank_ref[block, :, e : e + 1]).astype(F32)
            place_ref[block, e] = hit.astype(BF)
            if scaled:
                level_ref[block, e] = jnp.broadcast_to(
                    weight_ref[block, :, e : e + 1], (tokens, 128)
                )
    chunk = 256

    def body(step, carry):
        cols = pl.ds(pl.multiple_of(step * chunk, chunk), chunk)
        for block in range(blocks):
            acc = None
            for e in range(experts):
                part = matmul(
                    place_ref[block, e],
                    rows_refs[e][block * capacity : (block + 1) * capacity, cols],
                )
                if scaled:
                    part = part * jnp.concatenate(
                        [level_ref[block, e]] * (chunk // 128), axis=1
                    )
                acc = part if acc is None else acc + part
            outs[block][:, cols] = acc.astype(BF)
        return carry

    lax.fori_loop(0, outs[0].shape[1] // chunk, body, 0)


def spread(rows, rank, capacity, weight=None):
    blocks, tokens, experts = rank.shape
    operands = list(rows) + [rank] + ([] if weight is None else [weight])
    shape = jax.ShapeDtypeStruct((tokens, rows[0].shape[1]), BF)
    return pl.pallas_call(
        functools.partial(spread_kernel, experts, capacity, int(weight is not None)),
        in_specs=[pl.BlockSpec(memory_space=pltpu.VMEM)] * len(operands),
        out_specs=[pl.BlockSpec(memory_space=pltpu.VMEM)] * blocks,
        out_shape=[shape] * blocks,
        scratch_shapes=[
            pltpu.VMEM((blocks, experts, tokens, capacity), BF),
            pltpu.VMEM((blocks, experts, tokens, 128), F32),
        ],
        compiler_params=pltpu.CompilerParams(vmem_limit_bytes=48 << 20),
        cost_estimate=estimate(1 << 30, *operands, *operands),
    )(*operands)


def expert_kernel(x_ref, d_ref, w_ref, hidden_ref, joined_ref, back_ref):
    joined = matmul(x_ref[...], w_ref[...])
    gate, up = joined[:, :FF], joined[:, FF:]
    level = jax.nn.sigmoid(gate)
    active = gate * level
    grad = d_ref[...]
    hidden_ref[...] = (active * up).astype(BF)
    gate_back = (grad * up * level * (1.0 + gate * (1.0 - level))).astype(BF)
    up_back = (grad * active).astype(BF)
    joined_grad = jnp.concatenate([gate_back, up_back], axis=1)
    joined_ref[...] = joined_grad
    back_ref[...] = contract(joined_grad, w_ref[...], ((1,), (1,))).astype(BF)


def expert(rows, grad, weight):
    count = rows.shape[0]
    tile = min(256, count)

    def spec(n):
        return pl.BlockSpec((tile, n), lambda i: (i, 0))

    return pl.pallas_call(
        expert_kernel,
        grid=(count // tile,),
        in_specs=[spec(D), spec(FF), pl.BlockSpec(memory_space=pltpu.VMEM)],
        out_specs=[spec(FF), spec(2 * FF), spec(D)],
        out_shape=[
            jax.ShapeDtypeStruct((count, FF), BF),
            jax.ShapeDtypeStruct((count, 2 * FF), BF),
            jax.ShapeDtypeStruct((count, D), BF),
        ],
        compiler_params=pltpu.CompilerParams(vmem_limit_bytes=40 << 20),
        cost_estimate=estimate(2 * count * D * 4 * FF, rows, grad, weight),
    )(rows, grad, weight)


def result_kernel(hidden_ref, grad_ref, w_ref, out_ref, share_ref):
    out = matmul(hidden_ref[...], w_ref[...]).astype(BF)
    out_ref[...] = out
    share = jnp.sum(out.astype(F32) * grad_ref[...].astype(F32), axis=1, keepdims=True)
    share_ref[...] = jnp.broadcast_to(share, share_ref.shape)


def result(hidden, grad, weight):
    count = hidden.shape[0]
    tile = min(256, count)

    def spec(n):
        return pl.BlockSpec((tile, n), lambda i: (i, 0))

    out, share = pl.pallas_call(
        result_kernel,
        grid=(count // tile,),
        in_specs=[spec(FF), spec(D), pl.BlockSpec(memory_space=pltpu.VMEM)],
        out_specs=[spec(D), spec(128)],
        out_shape=[
            jax.ShapeDtypeStruct((count, D), BF),
            jax.ShapeDtypeStruct((count, 128), F32),
        ],
        compiler_params=pltpu.CompilerParams(vmem_limit_bytes=32 << 20),
        cost_estimate=estimate(2 * count * D * FF, grad, grad, weight),
    )(hidden, grad, weight)
    return out, share[:, 0]


def weight_grad_kernel(count, *refs):
    out_ref = refs[-1]
    acc = contract(refs[0][...], refs[count][...], ((0,), (0,)))
    for i in range(1, count):
        acc = acc + contract(refs[i][...], refs[count + i][...], ((0,), (0,)))
    out_ref[...] = acc


def weight_grad(lefts, rights, tile):
    count = len(lefts)
    m, n = lefts[0].shape[1], rights[0].shape[1]
    return pl.pallas_call(
        functools.partial(weight_grad_kernel, count),
        grid=(m // tile,),
        in_specs=[pl.BlockSpec((x.shape[0], tile), lambda i: (0, i)) for x in lefts]
        + [pl.BlockSpec(memory_space=pltpu.VMEM)] * count,
        out_specs=pl.BlockSpec((tile, n), lambda i: (i, 0)),
        out_shape=jax.ShapeDtypeStruct((m, n), F32),
        compiler_params=pltpu.CompilerParams(vmem_limit_bytes=48 << 20),
        cost_estimate=estimate(2 * m * n * count * lefts[0].shape[0], *rights, *rights, *lefts),
    )(*lefts, *rights)


def after(values, *others):
    return lax.optimization_barrier((values,) + others)[0]


def narrow(*parts):
    return total(*parts).astype(BF)


def build(sizes):
    nt, nr, nc = sizes["tok"], sizes["row"], sizes["col"]
    assert nt == 4 and nr == 4

    def tok(values, mask):
        return flip(values, "tok", mask, nt)

    def row(values, mask):
        return flip(values, "row", mask, nr)

    def col(values, mask):
        return flip(values, "col", mask, nc)

    def cols_of(values):
        return [values] + [col(values, m) for m in range(1, nc)]

    def plane_rows(own):
        half = own.shape[0] // 2
        ones, twos = row(own, 1), row(own, 2)
        threes = jnp.concatenate([row(twos[:half], 1), row(ones[half:], 2)])
        return [own, ones, twos, threes]

    def plane_gather(own):
        return jnp.stack(cols_of(jnp.stack(plane_rows(own))))

    def plane_scatter(parts):
        received = [col(parts[m], m) for m in range(1, nc)]
        mine = [narrow(parts[0][r], *[got[r] for got in received]) for r in range(nr)]
        half = mine[3].shape[0] // 2
        from_one = row(mine[3][:half], 1)
        from_two = row(mine[3][half:], 2)
        ones = jnp.concatenate([mine[1][:half], narrow(mine[1][half:], from_two)])
        twos = jnp.concatenate([narrow(mine[2][:half], from_one), mine[2][half:]])
        return total(mine[0], row(ones, 1), row(twos, 2))

    def gather16(own):
        base = [own, None, tok(own, 2), None]
        base[3] = tok(base[2], 1)
        base[1] = tok(after(own, base[2]), 1)
        out = {}
        prior = None
        for z in (0, 2, 3, 1):
            here = base[z] if prior is None else after(base[z], prior)
            ones, twos = row(here, 1), row(here, 2)
            threes = row(twos, 1) if z in (0, 2) else row(ones, 2)
            out[z] = [base[z], ones, twos, threes]
            prior = ones if z in (2, 3) else None
        return out

    def reduce_plane(parts, turn_at_one):
        ones, twos, threes = parts[1], parts[2], parts[3]
        if turn_at_one:
            ones = narrow(ones, row(threes, 2))
        else:
            twos = narrow(twos, row(threes, 1))
        return [parts[0], row(ones, 1), row(twos, 2)]

    def chain_tok(values):
        place = lax.axis_index("tok")
        inner = (place == 1) | (place == 2)
        inward = lax.ppermute(values, "tok", [(0, 1), (3, 2)])
        pair = lax.optimization_barrier(narrow(values, inward))
        whole = lax.optimization_barrier(narrow(pair, lax.ppermute(pair, "tok", [(1, 2), (2, 1)])))
        outward = lax.ppermute(whole, "tok", [(1, 0), (2, 3)])
        return jnp.where(inner, whole, outward).astype(F32)

    def sum_small(values):
        devices = nt * nr * nc
        length = values.shape[0]
        width = -(-length // (devices * 128)) * 128
        padded = jnp.concatenate([values, jnp.zeros((devices * width - length,), F32)])
        mine = jnp.sum(lax.all_to_all(padded.reshape(devices, width), ALL, 0, 0), axis=0)
        back = lax.all_to_all(jnp.broadcast_to(mine[None], (devices, width)), ALL, 0, 0)
        return back.reshape(-1)[:length]

    def per_device(
        hidden_in,
        seg_ids,
        expert_ids,
        norm1_gain,
        query_gain,
        key_gain,
        w_query,
        w_keyval,
        w_output,
        norm2_gain,
        router,
        w_gate_up,
        w_down,
        cotangent,
    ):
        return layer(
            hidden_in,
            seg_ids,
            expert_ids,
            norm1_gain,
            query_gain,
            key_gain,
            w_query,
            w_keyval,
            w_output,
            norm2_gain,
            router,
            w_gate_up,
            w_down,
            cotangent,
        )

    def layer(
        hidden_in,
        seg_ids,
        expert_ids,
        norm1_gain,
        query_gain,
        key_gain,
        w_query,
        w_keyval,
        w_output,
        norm2_gain,
        router,
        w_gate_up,
        w_down,
        cotangent,
    ):
        tok_i, row_i, col_i = (lax.axis_index(name) for name in ALL)
        experts = router.shape[1]
        tokens = hidden_in.shape[0]
        capacity = max(2, 2 * tokens * TOPK // experts)
        heads = HQ // (nr * nc)
        group_size = HQ // KV
        head_cols = heads * HD
        group = seg_ids.shape[1]
        key_cols = KV * HD
        all_cols = head_cols + 2 * HD
        row_block = D // nr
        width = w_keyval.shape[1]

        floats = hidden_in.astype(F32)
        normed = rms_scale(floats, norm1_gain).astype(BF)
        plane_norm = plane_rows(normed)
        keyval_cols = jnp.stack(cols_of(w_keyval))

        def head_block(first_col):
            return lax.dynamic_slice(
                keyval_cols,
                ((first_col // width) ^ col_i, 0, first_col % width),
                (1, row_block, HD),
            )[0]

        kv_heads = [((col_i * nr + (row_i ^ m)) * heads) // group_size for m in range(nr)]

        def weight_message(m):
            query_cols = lax.dynamic_slice_in_dim(w_query, (row_i ^ m) * head_cols, head_cols, 1)
            first = kv_heads[m] * HD
            return jnp.concatenate(
                [query_cols, head_block(first), head_block(key_cols + first)], axis=1
            )

        weight_qkv = jnp.zeros((D, all_cols), BF)
        for m in (3, 1, 2, 0):
            message = weight_message(m)
            message = row(message, m) if m else message
            weight_qkv = lax.dynamic_update_slice(
                weight_qkv, message, ((row_i ^ m) * row_block, 0)
            )
        seg_rows = seg_ids.astype(F32)
        seg_rel = jnp.concatenate([seg_rows] + [row(seg_rows, m) for m in range(1, nr)])
        col_order = jnp.arange(nc, dtype=jnp.int32) ^ col_i
        index_rel = col_order[:, None] * tokens + jnp.arange(tokens, dtype=jnp.int32)[None, :]
        index_rel = index_rel.reshape(group)
        seg_rel = jnp.take(seg_rel.reshape(nr, nc, tokens), col_order, axis=1).reshape(nr, group)
        allowed = (seg_rel[:, :, None] == seg_rel[:, None, :]) & (
            index_rel[None, None, :] <= index_rel[None, :, None]
        )
        mask = allowed.astype(F32)
        positions = jnp.sum(mask, axis=2) - 1.0
        frequency = ROPE_BASE ** (-(jnp.arange(HD // 2, dtype=F32) * 2.0 / HD))
        angles = positions[:, :, None] * frequency[None, None, :]
        cosine = jnp.concatenate([jnp.cos(angles)] * 2, axis=2)
        sine = jnp.sin(angles)
        sine = jnp.concatenate([-sine, sine], axis=2)

        chosen = jnp.any(
            expert_ids[:, :, None] == jnp.arange(experts, dtype=jnp.int32)[None, None, :], axis=1
        )
        below = (
            jnp.arange(tokens, dtype=jnp.int32)[:, None]
            > jnp.arange(tokens, dtype=jnp.int32)[None, :]
        )
        rank = jnp.where(chosen, matmul(below.astype(BF), chosen.astype(BF)), -1.0)
        relative = jnp.arange(nt * nr, dtype=jnp.int32)
        block_order = ((relative // nr) ^ tok_i) * nr + ((relative % nr) ^ row_i)

        def by_place(table):
            sent = table.T.reshape(nt * nr, nc * tokens)
            got = lax.all_to_all(sent, ("tok", "row"), 0, 0)
            got = jnp.take(got, block_order, axis=0).reshape(nt, nr, nc, tokens)
            return jnp.take(got, col_order, axis=2)

        rank_rows = by_place(after(rank, *plane_norm))
        rank_cols = rank_rows.transpose(0, 1, 3, 2)

        normed_all = jnp.stack(cols_of(jnp.stack(plane_norm))).reshape(nc * nr * tokens, D)
        raw = matmul(after(normed_all, mask, cosine, sine), weight_qkv).reshape(nc, nr, tokens, all_cols)

        cot_plane = plane_rows(cotangent)
        cot_two = [tok(part, 2) for part in cot_plane]
        cot_planes = {
            0: cot_plane,
            1: [tok(part, 1) for part in cot_plane],
            2: cot_two,
            3: [tok(part, 1) for part in cot_two],
        }

        qg, kg = query_gain[None], key_gain[None]
        mixed = attend(heads, raw, cosine, sine, mask, qg, kg)
        weight_out = jnp.zeros((head_cols, D), BF)
        for m in (3, 1, 2, 0):
            message = lax.dynamic_slice_in_dim(w_output, (row_i ^ m) * head_cols, head_cols, 0)
            message = after(row(message, m), mixed) if m else message
            weight_out = lax.dynamic_update_slice(
                weight_out, message, (0, (row_i ^ m) * row_block)
            )

        def by_col(values, weight, dims):
            return [
                contract(values[m].reshape(nr * tokens, -1), weight, dims)
                .astype(BF)
                .reshape(nr, tokens, -1)
                for m in range(nc)
            ]

        after_attn = floats + plane_scatter(by_col(mixed, weight_out, ((1,), (0,))))
        normed2 = rms_scale(after_attn, norm2_gain).astype(BF)
        row_planes = gather16(normed2)

        logits = matmul(normed2, router)
        raised = jnp.where(chosen, jnp.exp(logits), 0.0)
        gate = raised / jnp.sum(raised, axis=1, keepdims=True)
        gate_rows = by_place(gate)
        gate_cols = gate_rows.transpose(0, 1, 3, 2)

        def of_planes(table, planes):
            return jnp.concatenate([table[z] for z in planes])

        weight_gu, weight_down = w_gate_up[0], w_down[0]
        groups = ((2, 3), (0, 1))

        def exchange(picked):
            return [picked[0]] + [col(picked[m], m) for m in range(1, nc)]

        grad_in, hidden_grad = [], []
        for planes in groups:
            picked = exchange(
                pick(
                    [block for z in planes for block in cot_planes[z]],
                    of_planes(rank_rows, planes),
                    capacity,
                    of_planes(gate_rows, planes),
                ),
            )
            grad_in.append(picked)
            hidden_grad.append([contract(g, weight_down, ((1,), (1,))) for g in picked])

        expert_in, hidden, joined_grad, back = [], [], [], []
        share, mix = {}, []
        for i, planes in enumerate(groups):
            picked = exchange(
                pick(
                    after(
                        tuple(block for z in planes for block in row_planes[z]), *hidden_grad[i]
                    ),
                    of_planes(rank_rows, planes),
                    capacity,
                ),
            )
            expert_in.append(picked)
            hid, joined, results = [], [], []
            for m in range(nc):
                h, j, b = expert(picked[m], hidden_grad[i][m], weight_gu)
                hid.append(h)
                joined.append(j)
                results.append(b)
            hidden.append(hid)
            joined_grad.append(joined)
            back.append(spread(exchange(results), of_planes(rank_cols, planes), capacity))
            outs = []
            for m in range(nc):
                out, sums = result(after(hid[m], results[-1]), grad_in[i][m], weight_down)
                outs.append(out)
                for k, z in enumerate(planes):
                    share[m, z] = sums.reshape(len(planes), nr, capacity)[k]
            mix.append(
                spread(
                    exchange(outs),
                    of_planes(rank_cols, planes),
                    capacity,
                    of_planes(gate_cols, planes),
                )
            )

        far, near = back
        plane_two = reduce_plane(far[:4], False)
        plane_three = narrow(*reduce_plane(far[4:], True))
        plane_two = narrow(*plane_two, tok(plane_three, 1))
        plane_zero = reduce_plane(near[:4], False)
        plane_one = narrow(*reduce_plane(near[4:], True))
        rows_grad = total(*plane_zero, tok(plane_two, 2), tok(plane_one, 1))

        lefts = [x for part in expert_in for x in part]
        rights = [x for part in joined_grad for x in part]
        gate_up_grad = weight_grad(lefts, rights, 256)
        lefts = [x for part in hidden for x in part]
        rights = [x for part in grad_in for x in part]
        down_grad = weight_grad(lefts, rights, 256)

        share = jnp.stack([jnp.stack([share[m, z] for m in range(nc)], 1) for z in range(nt)])
        share = share.reshape(nt * nr, nc, capacity)
        share = jnp.take(jnp.take(share, block_order, axis=0), col_order, axis=1)
        share = lax.all_to_all(share.reshape(experts, capacity), ALL, 0, 0)
        slots = jnp.arange(capacity, dtype=jnp.int32).astype(F32)
        share = jnp.sum(
            jnp.where(rank[:, :, None] == slots[None, None, :], share[None], 0.0), axis=2
        )
        logit_grad = (share - gate * jnp.sum(share, axis=1, keepdims=True)).astype(BF)
        router_part = contract(normed2, logit_grad, ((0,), (0,)))
        normed2_grad = rows_grad + contract(logit_grad, router, ((1,), (1,)))

        grad_out = cotangent.astype(F32)
        _, norm2_back = jax.vjp(rms_scale, after_attn, norm2_gain)
        resid_grad, gain2_part = norm2_back(normed2_grad)
        resid_grad = resid_grad + grad_out
        out_grad = resid_grad.astype(BF)

        out_all = plane_gather(out_grad).reshape(nc * nr * tokens, D)
        mixed_grad = (
            contract(out_all, weight_out, ((1,), (1,))).astype(BF).reshape(mixed.shape)
        )
        output_part = contract(mixed.reshape(-1, head_cols), out_all, ((0,), (0,)))
        output_block = jnp.zeros((nr * head_cols, row_block), F32)
        for m in (0, 1, 2, 3):
            message = lax.dynamic_slice_in_dim(
                output_part, (row_i ^ m) * row_block, row_block, 1
            ).astype(BF)
            message = row(message, m) if m else message
            summed = chain_tok(message)
            output_block = lax.dynamic_update_slice(
                output_block, summed, ((row_i ^ m) * head_cols, 0)
            )

        qkv_send, qgain_part, kgain_part = attend_back(
            heads, raw, cosine, sine, mask, qg, kg, mixed, mixed_grad
        )
        normed_grad = plane_scatter(by_col(qkv_send, weight_qkv, ((1,), (1,))))
        _, norm1_back = jax.vjp(rms_scale, floats, norm1_gain)
        floats_grad, gain1_part = norm1_back(normed_grad)
        input_grad = (resid_grad + floats_grad).astype(BF)

        qkv_part = contract(normed_all, qkv_send.reshape(-1, all_cols), ((0,), (0,)))
        query_block = jnp.zeros((row_block, nr * head_cols), F32)
        full = jnp.zeros((row_block, 2 * key_cols), F32)
        for m in (0, 1, 2, 3):
            message = lax.dynamic_slice_in_dim(
                qkv_part, (row_i ^ m) * row_block, row_block, 0
            ).astype(BF)
            message = row(message, m) if m else message
            summed = chain_tok(message[:, :head_cols])
            query_block = lax.dynamic_update_slice(
                query_block, summed, (0, (row_i ^ m) * head_cols)
            )
            for half in range(2):
                start = half * key_cols + kv_heads[m] * HD
                first = head_cols + half * HD
                now = lax.dynamic_slice(full, (0, start), (row_block, HD))
                new = now + message[:, first : first + HD].astype(F32)
                full = lax.dynamic_update_slice(full, new, (0, start))
        pieces = [
            lax.dynamic_slice(full, (0, (col_i ^ m) * width), (row_block, width))
            for m in range(nc)
        ]
        keyval_mine = narrow(pieces[0], *[col(pieces[m].astype(BF), m) for m in range(1, nc)])
        keyval_block = chain_tok(keyval_mine)

        mix_three = narrow(*reduce_plane(mix[0][4:], True))
        mix_two = narrow(*reduce_plane(mix[0][:4], False), tok(mix_three, 1))
        mix_two = tok(mix_two, 2)
        late = [after(part, normed_grad) for part in mix[1]]
        mix_one = narrow(*reduce_plane(late[4:], True))
        mixture = total(
            *reduce_plane(late[:4], False), after(mix_two, normed_grad), tok(mix_one, 1)
        )
        layer_out = (after_attn + mixture).astype(BF)

        small = sum_small(
            jnp.concatenate(
                [
                    router_part.reshape(-1),
                    gain1_part,
                    gain2_part,
                    qgain_part.reshape(-1),
                    kgain_part.reshape(-1),
                ]
            )
        )
        edges = [0]
        for n in (D * experts, D, D, HD, HD):
            edges.append(edges[-1] + n)
        router_grad, norm1_grad, norm2_grad, query_gain_grad, key_gain_grad = (
            small[a:b] for a, b in zip(edges[:-1], edges[1:])
        )
        return (
            layer_out,
            input_grad,
            query_block,
            keyval_block,
            output_block,
            router_grad.reshape(D, experts),
            gate_up_grad[None],
            down_grad[None],
            norm1_grad,
            norm2_grad,
            query_gain_grad,
            key_gain_grad,
        )

    return per_device


def solution(mesh):
    by_all = P(ALL, None)
    by_expert = P(ALL, None, None)
    return jax.shard_map(
        build(dict(mesh.shape)),
        mesh=mesh,
        in_specs=(
            by_all,
            P(("tok", "row"), None),
            by_all,
            P(),
            P(),
            P(),
            P("row", "col"),
            P("row", "col"),
            P("col", "row"),
            P(),
            P(),
            by_expert,
            by_expert,
            by_all,
        ),
        out_specs=(
            by_all,
            by_all,
            P("row", "col"),
            P("row", "col"),
            P("col", "row"),
            P(),
            by_expert,
            by_expert,
            P(),
            P(),
            P(),
            P(),
        ),
        check_vma=False,
    )
```

profile of v0, /device:TPU:0, one launch (start us, length us, event | category | flops | bytes accessed | tf_op | source)
XLA Modules:
  0.0 1042.8 jit_solution(12216295210785813337)
XLA Ops:
  27.6 14.7 %collective-permute-done.2 = bf16[64,2048]{1,0:T(8,128)(2,1)S(1)} collective-permute-done((bf16[64,2048]{1,0:T(8,128)(2,1)S(1)}, bf16[64,2048]{1,0:T(8,128)(2,1)S(1)}, u32[]{:S(2)}, u32[]{:S(2)}) %collective-permute-start.2) | collective-permute-done | bytes 262176 | tf_op jit(solution)/shard_map/ppermute | solution.py:45
  53.5 12.3 %collective-permute-done.9 = bf16[512,768]{1,0:T(8,128)(2,1)S(1)} collective-permute-done((bf16[512,768]{1,0:T(8,128)(2,1)S(1)}, bf16[512,768]{1,0:T(8,128)(2,1)S(1)}, u32[]{:S(2)}, u32[]{:S(2)}) %collective-permute-start.9) | collective-permute-done | bytes 786464 | tf_op jit(solution)/shard_map/ppermute | solution.py:45
  67.5 15.0 %collective-permute-done.10 = bf16[512,768]{1,0:T(8,128)(2,1)S(1)} collective-permute-done((bf16[512,768]{1,0:T(8,128)(2,1)S(1)}, bf16[512,768]{1,0:T(8,128)(2,1)S(1)}, u32[]{:S(2)}, u32[]{:S(2)}) %collective-permute-start.10) | collective-permute-done | bytes 786464 | tf_op jit(solution)/shard_map/ppermute | solution.py:45
  90.9 11.6 %attend.1.mixed_ref = bf16[2,4,128,512]{3,2,1,0:T(8,128)(2,1)} custom-call(f32[2,4,128,768]{3,2,1,0:T(8,128)} %bitcast.261, f32[4,256,128]{2,1,0:T(8,128)} %pad_maximum_fusion.7.cos_ref, f32[4,256,128]{2,1,0:T(8,128)} %pad_maximum_fusion.8.sin_ref, f32[4,256,256]{2,1,0:T(8,128)} %and_convert_fusion.mask_ref, f32[1,128]{1,0:T(1,128)} %bitcast.255, ...), custom_call_target="tpu_custom_call" | custom-call | flops 4294967296 | bytes 4194304 | tf_op jit(solution)/shard_map/attend/pallas_call | solution.py:185
  120.4 6.8 collective-permute-done.32.refs_2_
  134.8 11.3 %collective-permute-done.16 = bf16[64,2048]{1,0:T(8,128)(2,1)S(1)} collective-permute-done((bf16[64,2048]{1,0:T(8,128)(2,1)S(1)}, bf16[64,2048]{1,0:T(8,128)(2,1)S(1)}, u32[]{:S(2)}, u32[]{:S(2)}) %collective-permute-start.16) | collective-permute-done | bytes 262176 | tf_op jit(solution)/shard_map/ppermute | solution.py:45
  175.3 29.3 %collective-permute-done.51.refs_1_ = bf16[128,2048]{1,0:T(8,128)(2,1)S(1)} collective-permute-done((bf16[128,2048]{1,0:T(8,128)(2,1)}, bf16[128,2048]{1,0:T(8,128)(2,1)S(1)}, u32[]{:S(2)}, u32[]{:S(2)}) %collective-permute-start.51) | collective-permute-done | bytes 524320 | tf_op jit(solution)/shard_map/ppermute | solution.py:45
  204.6 11.3 %collective-permute-done.52.refs_2_ = bf16[128,2048]{1,0:T(8,128)(2,1)S(1)} collective-permute-done((bf16[128,2048]{1,0:T(8,128)(2,1)}, bf16[128,2048]{1,0:T(8,128)(2,1)S(1)}, u32[]{:S(2)}, u32[]{:S(2)}) %collective-permute-start.52) | collective-permute-done | bytes 524320 | tf_op jit(solution)/shard_map/ppermute | solution.py:45
  216.0 6.6 collective-permute-done.53.refs_3_
  227.4 6.3 collective-permute-done.55.refs_5_
  233.6 11.3 %collective-permute-done.56.refs_6_ = bf16[128,2048]{1,0:T(8,128)(2,1)} collective-permute-done((bf16[128,2048]{1,0:T(8,128)(2,1)S(1)}, bf16[128,2048]{1,0:T(8,128)(2,1)}, u32[]{:S(2)}, u32[]{:S(2)}) %collective-permute-start.56) | collective-permute-done | bytes 524320 | tf_op jit(solution)/shard_map/ppermute | solution.py:45
  245.0 11.2 %collective-permute-done.57.refs_7_ = bf16[128,2048]{1,0:T(8,128)(2,1)} collective-permute-done((bf16[128,2048]{1,0:T(8,128)(2,1)S(1)}, bf16[128,2048]{1,0:T(8,128)(2,1)}, u32[]{:S(2)}, u32[]{:S(2)}) %collective-permute-start.57) | collective-permute-done | bytes 524320 | tf_op jit(solution)/shard_map/ppermute | solution.py:45
  256.2 5.8 shard_map.237
  262.7 10.0 collective-permute-done.36.refs_5_
  272.7 17.2 %collective-permute-done.37.refs_6_ = bf16[128,2048]{1,0:T(8,128)(2,1)} collective-permute-done((bf16[128,2048]{1,0:T(8,128)(2,1)}, bf16[128,2048]{1,0:T(8,128)(2,1)}, u32[]{:S(2)}, u32[]{:S(2)}) %collective-permute-start.37) | collective-permute-done | bytes 524320 | tf_op jit(solution)/shard_map/ppermute | solution.py:45
  289.9 5.7 collective-permute-done.38.refs_7_
  295.6 6.7 shard_map.229
  310.2 6.6 collective-permute-done.26.refs_1_
  324.3 6.3 collective-permute-done.24.refs_4_
  334.5 8.8 collective-permute-done.47.refs_3_
  349.0 7.8 collective-permute-done.48.refs_6_
  358.3 7.6 collective-permute-done.49.refs_7_
  382.7 6.3 collective-permute-done.22.refs_3_
  390.9 10.5 %collective-permute-done.30.refs_7_ = bf16[128,2048]{1,0:T(8,128)(2,1)S(1)} collective-permute-done((bf16[128,2048]{1,0:T(8,128)(2,1)}, bf16[128,2048]{1,0:T(8,128)(2,1)S(1)}, u32[]{:S(2)}, u32[]{:S(2)}) %collective-permute-start.30) | collective-permute-done | bytes 524320 | tf_op jit(solution)/shard_map/ppermute | solution.py:45
  401.4 6.1 shard_map.230
  413.3 7.6 shard_map.239
  427.3 7.2 shard_map.231
  437.8 9.4 shard_map.240
  464.4 9.5 shard_map.232
  474.0 5.3 shard_map.234
  493.1 7.2 shard_map.241
  502.9 17.7 %shard_map.245 = f32[2048,1536]{1,0:T(8,128)} custom-call(bf16[512,2048]{1,0:T(8,128)(2,1)} %get-tuple-element.157.x_ref.refs_0_, bf16[512,2048]{1,0:T(8,128)(2,1)} %collective-permute-done.59.x_ref.refs_1_, bf16[512,2048]{1,0:T(8,128)(2,1)} %get-tuple-element.132.x_ref.refs_2_, bf16[512,2048]{1,0:T(8,128)(2,1)} %collective-permute-done.40.x_ref.refs_3_, ...), custom_call_target="tpu_custom_call" | custom-call | flops 12884901888 | bytes 20971520 | tf_op jit(solution)/shard_map/pallas_call | solution.py:405
  523.8 5.9 shard_map.236
  537.5 20.6 %collective-permute-done.69 = bf16[128,2048]{1,0:T(8,128)(2,1)S(1)} collective-permute-done((bf16[128,2048]{1,0:T(8,128)(2,1)S(1)}, bf16[128,2048]{1,0:T(8,128)(2,1)S(1)}, u32[]{:S(2)}, u32[]{:S(2)}) %collective-permute-start.69) | collective-permute-done | bytes 524320 | tf_op jit(solution)/shard_map/ppermute | solution.py:45
  562.7 10.2 collective-permute-done.44
  574.5 18.9 %collective-permute-done.70 = bf16[128,2048]{1,0:T(8,128)(2,1)S(1)} collective-permute-done((bf16[128,2048]{1,0:T(8,128)(2,1)S(1)}, bf16[128,2048]{1,0:T(8,128)(2,1)S(1)}, u32[]{:S(2)}, u32[]{:S(2)}) %collective-permute-start.70) | collective-permute-done | bytes 524320 | tf_op jit(solution)/shard_map/ppermute | solution.py:45
  600.5 7.2 shard_map.244
  610.0 7.7 collective-permute-done.72
  626.3 11.6 %shard_map.246 = f32[768,2048]{1,0:T(8,128)} custom-call(bf16[512,768]{1,0:T(8,128)(2,1)S(1)} %copy-done.18, bf16[512,768]{1,0:T(8,128)(2,1)S(1)} %copy-done.23, bf16[512,768]{1,0:T(8,128)(2,1)S(1)} %copy-done.21, bf16[512,768]{1,0:T(8,128)(2,1)S(1)} %copy-done.25, bf16[512,2048]{1,0:T(8,128)(2,1)S(1)} %copy-done.7, ...), custom_call_target="tpu_custom_call" | custom-call | flops 6442450944 | bytes 19922944 | tf_op jit(solution)/shard_map/pallas_call | solution.py:405
  649.3 6.1 collective-permute-done.76
  666.5 12.1 %collective-permute-done.91 = bf16[128,2048]{1,0:T(8,128)(2,1)S(1)} collective-permute-done((bf16[128,2048]{1,0:T(8,128)(2,1)S(1)}, bf16[128,2048]{1,0:T(8,128)(2,1)S(1)}, u32[]{:S(2)}, u32[]{:S(2)}) %collective-permute-start.91) | collective-permute-done | bytes 524320 | tf_op jit(solution)/shard_map/ppermute | solution.py:45
  681.5 7.3 shard_map.235
  697.7 15.8 %attend_back.1 = (bf16[2,4,128,768]{3,2,1,0:T(8,128)(2,1)}, f32[1,128]{1,0:T(1,128)}, f32[1,128]{1,0:T(1,128)}) custom-call(f32[2,4,128,768]{3,2,1,0:T(8,128)} %bitcast.262, f32[4,256,128]{2,1,0:T(8,128)} %pad_maximum_fusion.7.cos_ref, f32[4,256,128]{2,1,0:T(8,128)} %pad_maximum_fusion.8.sin_ref, f32[4,256,256]{2,1,0:T(8,128)} %and_convert_fusion.mask_ref, ...), custom_call_target="tpu_custom_call" | custom-call | flops 6442450944 | bytes 7340032 | tf_op jit(solution)/shard_map/attend_back/pallas_call | solution.py:198
  715.6 5.7 convolution_bitcast_fusion
  736.9 6.8 collective-permute-done.99
  754.2 11.0 %collective-permute-done.106 = bf16[512,768]{1,0:T(8,128)(2,1)S(1)} collective-permute-done((bf16[512,768]{1,0:T(8,128)(2,1)S(1)}, bf16[512,768]{1,0:T(8,128)(2,1)S(1)}, u32[]{:S(2)}, u32[]{:S(2)}) %collective-permute-start.106) | collective-permute-done | bytes 786464 | tf_op jit(solution)/shard_map/ppermute | solution.py:45
  770.9 9.1 collective-permute-done.121
  788.6 10.5 %collective-permute-start.130 = (bf16[512,512]{1,0:T(8,128)(2,1)S(1)}, bf16[512,512]{1,0:T(8,128)(2,1)S(1)}, u32[]{:S(2)}, u32[]{:S(2)}) collective-permute-start(bf16[512,512]{1,0:T(8,128)(2,1)S(1)} %collective-permute-done.129), channel_id=1, source_target_pairs={{0,8},{24,16},{1,9},{25,17},{2,10},{26,18},{3,11},{27,19},{4,12},{... | collective-permute-start | bytes 1572872 | tf_op jit(solution)/shard_map/ppermute | solution.py:485
  800.9 6.5 collective-permute-done.126
  812.0 6.7 collective-permute-done.130
  823.2 6.7 collective-permute-done.103
  830.0 11.1 %collective-permute-done.107 = bf16[512,512]{1,0:T(8,128)(2,1)S(1)} collective-permute-done((bf16[512,512]{1,0:T(8,128)(2,1)S(1)}, bf16[512,512]{1,0:T(8,128)(2,1)S(1)}, u32[]{:S(2)}, u32[]{:S(2)}) %collective-permute-start.107) | collective-permute-done | bytes 524320 | tf_op jit(solution)/shard_map/ppermute | solution.py:485
  841.9 6.9 collective-permute-done.111
  854.3 9.4 collective-permute-done.101
  868.1 9.0 collective-permute-done.120
  878.5 17.3 %collective-permute-start.115 = (bf16[512,512]{1,0:T(8,128)(2,1)S(1)}, bf16[512,512]{1,0:T(8,128)(2,1)S(1)}, u32[]{:S(2)}, u32[]{:S(2)}) collective-permute-start(bf16[512,512]{1,0:T(8,128)(2,1)S(1)} %add_convert_fusion.10), channel_id=1, source_target_pairs={{0,8},{24,16},{1,9},{25,17},{2,10},{26,18},{3,11},{27,19},{4,12},{... | collective-permute-start | bytes 1572872 | tf_op jit(solution)/shard_map/ppermute | solution.py:485
  905.8 8.9 collective-permute-done.124
  916.1 11.1 %collective-permute-done.128 = bf16[512,512]{1,0:T(8,128)(2,1)S(1)} collective-permute-done((bf16[512,512]{1,0:T(8,128)(2,1)S(1)}, bf16[512,512]{1,0:T(8,128)(2,1)S(1)}, u32[]{:S(2)}, u32[]{:S(2)}) %collective-permute-start.128) | collective-permute-done | bytes 524320 | tf_op jit(solution)/shard_map/ppermute | solution.py:488
  928.7 9.8 collective-permute-done.132
  938.4 5.3 collective-permute-start.81
  951.3 5.2 collective-permute-done.79
  965.7 6.4 collective-permute-done.113
  986.8 8.2 all-to-all-start.3
  1022.6 5.6 all-to-all-done.4
  (656 shorter events, 421.9 us)
Async XLA Ops:
  20.9 81.6 %collective-permute-start.12 = (bf16[512,512]{1,0:T(8,128)(2,1)}, bf16[512,512]{1,0:T(8,128)(2,1)}, u32[]{:S(2)}, u32[]{:S(2)}) collective-permute-start(bf16[512,512]{1,0:T(8,128)(2,1)} %get-tuple-element.312), channel_id=1, source_target_pairs={{0,6},{2,4},{4,2},{6,0},{1,7},{3,5},{5,3},{7,1},{8,14},{10,12},{12... | collective-permute-start | bytes 1572872 | tf_op jit(solution)/shard_map/ppermute | solution.py:45
  43.9 39.5 %collective-permute-start.4 = (bf16[4,128,2048]{2,1,0:T(8,128)(2,1)S(1)}, bf16[4,128,2048]{2,1,0:T(8,128)(2,1)S(1)}, u32[]{:S(2)}, u32[]{:S(2)}) collective-permute-start(bf16[4,128,2048]{2,1,0:T(8,128)(2,1)S(1)} %get-tuple-element.318), channel_id=1, source_target_pairs={{0,1},{1,0},{2,3},{3,2},{4,5},{5,4},{6,7},{7,6},{8,9},{9,8},{10,11... | collective-permute-start | bytes 6291464 | tf_op jit(solution)/shard_map/ppermute | solution.py:45
  47.0 35.5 %collective-permute-start.10 = (bf16[512,768]{1,0:T(8,128)(2,1)S(1)}, bf16[512,768]{1,0:T(8,128)(2,1)S(1)}, u32[]{:S(2)}, u32[]{:S(2)}) collective-permute-start(bf16[512,768]{1,0:T(8,128)(2,1)S(1)} %pad_maximum_fusion.5), channel_id=1, source_target_pairs={{0,2},{2,0},{4,6},{6,4},{1,3},{3,1},{5,7},{7,5},{8,10},{10,8},{12,... | collective-permute-start | bytes 2359304 | tf_op jit(solution)/shard_map/ppermute | solution.py:45
  47.7 35.6 %collective-permute-start.11 = (bf16[512,768]{1,0:T(8,128)(2,1)S(1)}, bf16[512,768]{1,0:T(8,128)(2,1)S(1)}, u32[]{:S(2)}, u32[]{:S(2)}) collective-permute-start(bf16[512,768]{1,0:T(8,128)(2,1)S(1)} %pad_maximum_fusion.6), channel_id=1, source_target_pairs={{0,4},{2,6},{4,0},{6,2},{1,5},{3,7},{5,1},{7,3},{8,12},{10,14},{12... | collective-permute-start | bytes 2359304 | tf_op jit(solution)/shard_map/ppermute | solution.py:45
  65.8 36.7 %collective-permute-start.13 = (bf16[512,512]{1,0:T(8,128)(2,1)S(1)}, bf16[512,512]{1,0:T(8,128)(2,1)S(1)}, u32[]{:S(2)}, u32[]{:S(2)}) collective-permute-start(bf16[512,512]{1,0:T(8,128)(2,1)S(1)} %copy-done.71), channel_id=1, source_target_pairs={{0,2},{2,0},{4,6},{6,4},{1,3},{3,1},{5,7},{7,5},{8,10},{10,8},{12,... | collective-permute-start | bytes 1572872 | tf_op jit(solution)/shard_map/ppermute | solution.py:45
  109.0 62.9 %collective-permute-start.50 = (bf16[128,2048]{1,0:T(8,128)(2,1)}, bf16[128,2048]{1,0:T(8,128)(2,1)S(1)}, u32[]{:S(2)}, u32[]{:S(2)}) collective-permute-start(bf16[128,2048]{1,0:T(8,128)(2,1)} %refs_0_.1), channel_id=1, source_target_pairs={{0,16},{8,24},{16,0},{24,8},{1,17},{9,25},{17,1},{25,9},{2,18},{10... | collective-permute-start | bytes 1572872 | tf_op jit(solution)/shard_map/ppermute | solution.py:45
  133.4 25.7 %collective-permute-start.19 = (bf16[128,2048]{1,0:T(8,128)(2,1)S(1)}, bf16[128,2048]{1,0:T(8,128)(2,1)}, u32[]{:S(2)}, u32[]{:S(2)}) collective-permute-start(bf16[128,2048]{1,0:T(8,128)(2,1)S(1)} %pad_maximum_fusion.10), channel_id=1, source_target_pairs={{0,4},{2,6},{4,0},{6,2},{1,5},{3,7},{5,1},{7,3},{8,12},{10,14},{12... | collective-permute-start | bytes 1572872 | tf_op jit(solution)/shard_map/ppermute | solution.py:45
  152.4 109.8 %collective-permute-start.35 = (bf16[128,2048]{1,0:T(8,128)(2,1)}, bf16[128,2048]{1,0:T(8,128)(2,1)}, u32[]{:S(2)}, u32[]{:S(2)}) collective-permute-start(bf16[128,2048]{1,0:T(8,128)(2,1)} %refs_0_.1), channel_id=1, source_target_pairs={{0,8},{8,0},{16,24},{24,16},{1,9},{9,1},{17,25},{25,17},{2,10},{10... | collective-permute-start | bytes 1572872 | tf_op jit(solution)/shard_map/ppermute | solution.py:45
  155.9 48.7 %collective-permute-start.51 = (bf16[128,2048]{1,0:T(8,128)(2,1)}, bf16[128,2048]{1,0:T(8,128)(2,1)S(1)}, u32[]{:S(2)}, u32[]{:S(2)}) collective-permute-start(bf16[128,2048]{1,0:T(8,128)(2,1)} %collective-permute-done.31.refs_1_), channel_id=1, source_target_pairs={{0,16},{8,24},{16,0},{24,8},{1,17},{9,25},{17,1},{25,9},{2,18},{10... | collective-permute-start | bytes 1572872 | tf_op jit(solution)/shard_map/ppermute | solution.py:45
  159.1 56.9 %collective-permute-start.52 = (bf16[128,2048]{1,0:T(8,128)(2,1)}, bf16[128,2048]{1,0:T(8,128)(2,1)S(1)}, u32[]{:S(2)}, u32[]{:S(2)}) collective-permute-start(bf16[128,2048]{1,0:T(8,128)(2,1)} %collective-permute-done.32.refs_2_), channel_id=1, source_target_pairs={{0,16},{8,24},{16,0},{24,8},{1,17},{9,25},{17,1},{25,9},{2,18},{10... | collective-permute-start | bytes 1572872 | tf_op jit(solution)/shard_map/ppermute | solution.py:45
  159.6 63.0 %collective-permute-start.53 = (bf16[128,2048]{1,0:T(8,128)(2,1)}, bf16[128,2048]{1,0:T(8,128)(2,1)S(1)}, u32[]{:S(2)}, u32[]{:S(2)}) collective-permute-start(bf16[128,2048]{1,0:T(8,128)(2,1)} %constant_dynamic-update-slice_fusion.8.refs_3_), channel_id=1, source_target_pairs={{0,16},{8,24},{16,0},{24,8},{1,17},{9,25},{17,1},{25,9},{2,18},{10... | collective-permute-start | bytes 1572872 | tf_op jit(solution)/shard_map/ppermute | solution.py:45
  167.9 56.5 %all-to-all-start.1 = ((f32[16,1,256]{2,1,0:T(1,128)}), f32[16,1,256]{2,1,0:T(1,128)S(1)}, u32[]{:S(2)}, u32[]{:S(2)}) async-start(f32[16,1,256]{2,1,0:T(1,128)} %bitcast.39), calls=%async_computation.1 | async-start | bytes 32768 | tf_op jit(solution)/shard_map/all_to_all | solution.py:620
  171.9 54.8 %collective-permute-start.54 = (bf16[128,2048]{1,0:T(8,128)(2,1)S(1)}, bf16[128,2048]{1,0:T(8,128)(2,1)S(1)}, u32[]{:S(2)}, u32[]{:S(2)}) collective-permute-start(bf16[128,2048]{1,0:T(8,128)(2,1)S(1)} %collective-permute-done.50.refs_0_), channel_id=1, source_target_pairs={{0,8},{8,0},{16,24},{24,16},{1,9},{9,1},{17,25},{25,17},{2,10},{10... | collective-permute-start | bytes 1572872 | tf_op jit(solution)/shard_map/ppermute | solution.py:45
  204.6 29.0 %collective-permute-start.55 = (bf16[128,2048]{1,0:T(8,128)(2,1)S(1)}, bf16[128,2048]{1,0:T(8,128)(2,1)S(1)}, u32[]{:S(2)}, u32[]{:S(2)}) collective-permute-start(bf16[128,2048]{1,0:T(8,128)(2,1)S(1)} %collective-permute-done.51.refs_1_), channel_id=1, source_target_pairs={{0,8},{8,0},{16,24},{24,16},{1,9},{9,1},{17,25},{25,17},{2,10},{10... | collective-permute-start | bytes 1572872 | tf_op jit(solution)/shard_map/ppermute | solution.py:45
  216.0 29.0 %collective-permute-start.56 = (bf16[128,2048]{1,0:T(8,128)(2,1)S(1)}, bf16[128,2048]{1,0:T(8,128)(2,1)}, u32[]{:S(2)}, u32[]{:S(2)}) collective-permute-start(bf16[128,2048]{1,0:T(8,128)(2,1)S(1)} %collective-permute-done.52.refs_2_), channel_id=1, source_target_pairs={{0,8},{8,0},{16,24},{24,16},{1,9},{9,1},{17,25},{25,17},{2,10},{10... | collective-permute-start | bytes 1572872 | tf_op jit(solution)/shard_map/ppermute | solution.py:45
  222.6 33.7 %collective-permute-start.57 = (bf16[128,2048]{1,0:T(8,128)(2,1)S(1)}, bf16[128,2048]{1,0:T(8,128)(2,1)}, u32[]{:S(2)}, u32[]{:S(2)}) collective-permute-start(bf16[128,2048]{1,0:T(8,128)(2,1)S(1)} %collective-permute-done.53.refs_3_), channel_id=1, source_target_pairs={{0,8},{8,0},{16,24},{24,16},{1,9},{9,1},{17,25},{25,17},{2,10},{10... | collective-permute-start | bytes 1572872 | tf_op jit(solution)/shard_map/ppermute | solution.py:45
  226.7 46.0 %collective-permute-start.36 = (bf16[128,2048]{1,0:T(8,128)(2,1)}, bf16[128,2048]{1,0:T(8,128)(2,1)}, u32[]{:S(2)}, u32[]{:S(2)}) collective-permute-start(bf16[128,2048]{1,0:T(8,128)(2,1)} %collective-permute-done.31.refs_1_), channel_id=1, source_target_pairs={{0,8},{8,0},{16,24},{24,16},{1,9},{9,1},{17,25},{25,17},{2,10},{10... | collective-permute-start | bytes 1572872 | tf_op jit(solution)/shard_map/ppermute | solution.py:45
  233.6 56.3 %collective-permute-start.37 = (bf16[128,2048]{1,0:T(8,128)(2,1)}, bf16[128,2048]{1,0:T(8,128)(2,1)}, u32[]{:S(2)}, u32[]{:S(2)}) collective-permute-start(bf16[128,2048]{1,0:T(8,128)(2,1)} %collective-permute-done.32.refs_2_), channel_id=1, source_target_pairs={{0,8},{8,0},{16,24},{24,16},{1,9},{9,1},{17,25},{25,17},{2,10},{10... | collective-permute-start | bytes 1572872 | tf_op jit(solution)/shard_map/ppermute | solution.py:45
  245.0 50.7 %collective-permute-start.38 = (bf16[128,2048]{1,0:T(8,128)(2,1)}, bf16[128,2048]{1,0:T(8,128)(2,1)}, u32[]{:S(2)}, u32[]{:S(2)}) collective-permute-start(bf16[128,2048]{1,0:T(8,128)(2,1)} %constant_dynamic-update-slice_fusion.8.refs_3_), channel_id=1, source_target_pairs={{0,8},{8,0},{16,24},{24,16},{1,9},{9,1},{17,25},{25,17},{2,10},{10... | collective-permute-start | bytes 1572872 | tf_op jit(solution)/shard_map/ppermute | solution.py:45
  262.0 81.9 %collective-permute-start.58 = (bf16[512,2048]{1,0:T(8,128)(2,1)}, bf16[512,2048]{1,0:T(8,128)(2,1)}, u32[]{:S(2)}, u32[]{:S(2)}) collective-permute-start(bf16[512,2048]{1,0:T(8,128)(2,1)} %get-tuple-element.148), channel_id=1, source_target_pairs={{0,1},{1,0},{2,3},{3,2},{4,5},{5,4},{6,7},{7,6},{8,9},{9,8},{10,11... | collective-permute-start | bytes 6291464 | tf_op jit(solution)/shard_map/ppermute | solution.py:45
  262.3 40.1 %collective-permute-start.23 = (bf16[128,2048]{1,0:T(8,128)(2,1)}, bf16[128,2048]{1,0:T(8,128)(2,1)S(1)}, u32[]{:S(2)}, u32[]{:S(2)}) collective-permute-start(bf16[128,2048]{1,0:T(8,128)(2,1)} %multiply_convert_fusion.refs_0_), channel_id=1, source_target_pairs={{0,16},{8,24},{16,0},{24,8},{1,17},{9,25},{17,1},{25,9},{2,18},{10... | collective-permute-start | bytes 1572872 | tf_op jit(solution)/shard_map/ppermute | solution.py:45
  302.3 75.0 %collective-permute-start.39 = (bf16[512,2048]{1,0:T(8,128)(2,1)}, bf16[512,2048]{1,0:T(8,128)(2,1)}, u32[]{:S(2)}, u32[]{:S(2)}) collective-permute-start(bf16[512,2048]{1,0:T(8,128)(2,1)} %get-tuple-element.123), channel_id=1, source_target_pairs={{0,1},{1,0},{2,3},{3,2},{4,5},{5,4},{6,7},{7,6},{8,9},{9,8},{10,11... | collective-permute-start | bytes 6291464 | tf_op jit(solution)/shard_map/ppermute | solution.py:45
  330.6 43.9 %collective-permute-start.21 = (bf16[128,2048]{1,0:T(8,128)(2,1)}, bf16[128,2048]{1,0:T(8,128)(2,1)}, u32[]{:S(2)}, u32[]{:S(2)}) collective-permute-start(bf16[128,2048]{1,0:T(8,128)(2,1)} %multiply_convert_fusion.refs_0_), channel_id=1, source_target_pairs={{0,4},{2,6},{4,0},{6,2},{1,5},{3,7},{5,1},{7,3},{8,12},{10,14},{12... | collective-permute-start | bytes 1572872 | tf_op jit(solution)/shard_map/ppermute | solution.py:45
  343.3 32.6 %collective-permute-start.28 = (bf16[128,2048]{1,0:T(8,128)(2,1)}, bf16[128,2048]{1,0:T(8,128)(2,1)}, u32[]{:S(2)}, u32[]{:S(2)}) collective-permute-start(bf16[128,2048]{1,0:T(8,128)(2,1)} %collective-permute-done.24.refs_4_), channel_id=1, source_target_pairs={{0,2},{2,0},{4,6},{6,4},{1,3},{3,1},{5,7},{7,5},{8,10},{10,8},{12,... | collective-permute-start | bytes 1572872 | tf_op jit(solution)/shard_map/ppermute | solution.py:45
  356.8 25.9 %collective-permute-start.20 = (bf16[128,2048]{1,0:T(8,128)(2,1)}, bf16[128,2048]{1,0:T(8,128)(2,1)}, u32[]{:S(2)}, u32[]{:S(2)}) collective-permute-start(bf16[128,2048]{1,0:T(8,128)(2,1)} %multiply_convert_fusion.refs_0_), channel_id=1, source_target_pairs={{0,2},{2,0},{4,6},{6,4},{1,3},{3,1},{5,7},{7,5},{8,10},{10,8},{12,... | collective-permute-start | bytes 1572872 | tf_op jit(solution)/shard_map/ppermute | solution.py:45
  370.3 67.6 %collective-permute-start.59 = (bf16[512,2048]{1,0:T(8,128)(2,1)}, bf16[512,2048]{1,0:T(8,128)(2,1)}, u32[]{:S(2)}, u32[]{:S(2)}) collective-permute-start(bf16[512,2048]{1,0:T(8,128)(2,1)} %get-tuple-element.159), channel_id=1, source_target_pairs={{0,1},{1,0},{2,3},{3,2},{4,5},{5,4},{6,7},{7,6},{8,9},{9,8},{10,11... | collective-permute-start | bytes 6291464 | tf_op jit(solution)/shard_map/ppermute | solution.py:45
  407.5 52.7 %collective-permute-start.40 = (bf16[512,2048]{1,0:T(8,128)(2,1)}, bf16[512,2048]{1,0:T(8,128)(2,1)}, u32[]{:S(2)}, u32[]{:S(2)}) collective-permute-start(bf16[512,2048]{1,0:T(8,128)(2,1)} %get-tuple-element.134), channel_id=1, source_target_pairs={{0,1},{1,0},{2,3},{3,2},{4,5},{5,4},{6,7},{7,6},{8,9},{9,8},{10,11... | collective-permute-start | bytes 6291464 | tf_op jit(solution)/shard_map/ppermute | solution.py:45
  447.2 44.8 %collective-permute-start.60 = (bf16[512,2048]{1,0:T(8,128)(2,1)}, bf16[512,2048]{1,0:T(8,128)(2,1)}, u32[]{:S(2)}, u32[]{:S(2)}) collective-permute-start(bf16[512,2048]{1,0:T(8,128)(2,1)} %get-tuple-element.160), channel_id=1, source_target_pairs={{0,1},{1,0},{2,3},{3,2},{4,5},{5,4},{6,7},{7,6},{8,9},{9,8},{10,11... | collective-permute-start | bytes 6291464 | tf_op jit(solution)/shard_map/ppermute | solution.py:45
  459.5 140.9 %collective-permute-start.86 = (bf16[512,2048]{1,0:T(8,128)(2,1)}, bf16[512,2048]{1,0:T(8,128)(2,1)}, u32[]{:S(2)}, u32[]{:S(2)}) collective-permute-start(bf16[512,2048]{1,0:T(8,128)(2,1)} %copy-done.28), channel_id=1, source_target_pairs={{0,1},{1,0},{2,3},{3,2},{4,5},{5,4},{6,7},{7,6},{8,9},{9,8},{10,11... | collective-permute-start | bytes 6291464 | tf_op jit(solution)/shard_map/ppermute | solution.py:45
  474.0 49.8 %collective-permute-start.42 = (bf16[512,2048]{1,0:T(8,128)(2,1)}, bf16[512,2048]{1,0:T(8,128)(2,1)}, u32[]{:S(2)}, u32[]{:S(2)}) collective-permute-start(bf16[512,2048]{1,0:T(8,128)(2,1)} %get-tuple-element.135), channel_id=1, source_target_pairs={{0,1},{1,0},{2,3},{3,2},{4,5},{5,4},{6,7},{7,6},{8,9},{9,8},{10,11... | collective-permute-start | bytes 6291464 | tf_op jit(solution)/shard_map/ppermute | solution.py:45
  488.4 32.2 %all-to-all-start.2 = ((f32[32,1,64]{2,1,0:T(1,128)}), f32[32,1,64]{2,1,0:T(1,128)S(1)}, u32[]{:S(2)}, u32[]{:S(2)}) async-start(f32[32,1,64]{2,1,0:T(1,128)} %bitcast.67), calls=%async_computation.2 | async-start | bytes 32768 | tf_op jit(solution)/shard_map/all_to_all | solution.py:744
  501.1 30.2 %collective-permute-start.64 = (bf16[128,2048]{1,0:T(8,128)(2,1)}, bf16[128,2048]{1,0:T(8,128)(2,1)}, u32[]{:S(2)}, u32[]{:S(2)}) collective-permute-start(bf16[128,2048]{1,0:T(8,128)(2,1)} %get-tuple-element.167), channel_id=1, source_target_pairs={{0,4},{2,6},{4,0},{6,2},{1,5},{3,7},{5,1},{7,3},{8,12},{10,14},{12... | collective-permute-start | bytes 1572872 | tf_op jit(solution)/shard_map/ppermute | solution.py:45
  521.7 38.0 %collective-permute-start.66 = (bf16[128,2048]{1,0:T(8,128)(2,1)}, bf16[128,2048]{1,0:T(8,128)(2,1)S(1)}, u32[]{:S(2)}, u32[]{:S(2)}) collective-permute-start(bf16[128,2048]{1,0:T(8,128)(2,1)} %get-tuple-element.168), channel_id=1, source_target_pairs={{0,4},{2,6},{4,0},{6,2},{1,5},{3,7},{5,1},{7,3},{8,12},{10,14},{12... | collective-permute-start | bytes 1572872 | tf_op jit(solution)/shard_map/ppermute | solution.py:45
  529.7 32.3 %collective-permute-start.71 = (bf16[128,2048]{1,0:T(8,128)(2,1)S(1)}, bf16[128,2048]{1,0:T(8,128)(2,1)S(1)}, u32[]{:S(2)}, u32[]{:S(2)}) collective-permute-start(bf16[128,2048]{1,0:T(8,128)(2,1)S(1)} %get-tuple-element.172), channel_id=1, source_target_pairs={{0,4},{2,6},{4,0},{6,2},{1,5},{3,7},{5,1},{7,3},{8,12},{10,14},{12... | collective-permute-start | bytes 1572872 | tf_op jit(solution)/shard_map/ppermute | solution.py:45
  531.3 26.8 %collective-permute-start.69 = (bf16[128,2048]{1,0:T(8,128)(2,1)S(1)}, bf16[128,2048]{1,0:T(8,128)(2,1)S(1)}, u32[]{:S(2)}, u32[]{:S(2)}) collective-permute-start(bf16[128,2048]{1,0:T(8,128)(2,1)S(1)} %get-tuple-element.171), channel_id=1, source_target_pairs={{0,4},{2,6},{4,0},{6,2},{1,5},{3,7},{5,1},{7,3},{8,12},{10,14},{12... | collective-permute-start | bytes 1572872 | tf_op jit(solution)/shard_map/ppermute | solution.py:45
  559.7 35.4 %collective-permute-start.61 = (bf16[128,2048]{1,0:T(8,128)(2,1)S(1)}, bf16[128,2048]{1,0:T(8,128)(2,1)S(1)}, u32[]{:S(2)}, u32[]{:S(2)}) collective-permute-start(bf16[128,2048]{1,0:T(8,128)(2,1)S(1)} %copy-done.34), channel_id=1, source_target_pairs={{0,2},{2,0},{4,6},{6,4},{1,3},{3,1},{5,7},{7,5},{8,10},{10,8},{12,... | collective-permute-start | bytes 1572872 | tf_op jit(solution)/shard_map/ppermute | solution.py:45
  560.3 33.0 %collective-permute-start.70 = (bf16[128,2048]{1,0:T(8,128)(2,1)S(1)}, bf16[128,2048]{1,0:T(8,128)(2,1)S(1)}, u32[]{:S(2)}, u32[]{:S(2)}) collective-permute-start(bf16[128,2048]{1,0:T(8,128)(2,1)S(1)} %add_convert_fusion.28), channel_id=1, source_target_pairs={{0,2},{2,0},{4,6},{6,4},{1,3},{3,1},{5,7},{7,5},{8,10},{10,8},{12,... | collective-permute-start | bytes 1572872 | tf_op jit(solution)/shard_map/ppermute | solution.py:45
  562.1 33.7 %collective-permute-start.63 = (bf16[128,2048]{1,0:T(8,128)(2,1)S(1)}, bf16[128,2048]{1,0:T(8,128)(2,1)S(1)}, u32[]{:S(2)}, u32[]{:S(2)}) collective-permute-start(bf16[128,2048]{1,0:T(8,128)(2,1)S(1)} %add_convert_fusion.32), channel_id=1, source_target_pairs={{0,4},{2,6},{4,0},{6,2},{1,5},{3,7},{5,1},{7,3},{8,12},{10,14},{12... | collective-permute-start | bytes 1572872 | tf_op jit(solution)/shard_map/ppermute | solution.py:45
  600.4 81.1 %collective-permute-start.41 = (bf16[512,2048]{1,0:T(8,128)(2,1)}, bf16[512,2048]{1,0:T(8,128)(2,1)}, u32[]{:S(2)}, u32[]{:S(2)}) collective-permute-start(bf16[512,2048]{1,0:T(8,128)(2,1)} %get-tuple-element.140), channel_id=1, source_target_pairs={{0,1},{1,0},{2,3},{3,2},{4,5},{5,4},{6,7},{7,6},{8,9},{9,8},{10,11... | collective-permute-start | bytes 6291464 | tf_op jit(solution)/shard_map/ppermute | solution.py:45
  608.5 39.0 %collective-permute-start.90 = (bf16[128,2048]{1,0:T(8,128)(2,1)}, bf16[128,2048]{1,0:T(8,128)(2,1)}, u32[]{:S(2)}, u32[]{:S(2)}) collective-permute-start(bf16[128,2048]{1,0:T(8,128)(2,1)} %get-tuple-element.197), channel_id=1, source_target_pairs={{0,4},{2,6},{4,0},{6,2},{1,5},{3,7},{5,1},{7,3},{8,12},{10,14},{12... | collective-permute-start | bytes 1572872 | tf_op jit(solution)/shard_map/ppermute | solution.py:45
  655.4 33.4 %collective-permute-start.87 = (bf16[128,2048]{1,0:T(8,128)(2,1)}, bf16[128,2048]{1,0:T(8,128)(2,1)S(1)}, u32[]{:S(2)}, u32[]{:S(2)}) collective-permute-start(bf16[128,2048]{1,0:T(8,128)(2,1)} %get-tuple-element.192), channel_id=1, source_target_pairs={{0,2},{2,0},{4,6},{6,4},{1,3},{3,1},{5,7},{7,5},{8,10},{10,8},{12,... | collective-permute-start | bytes 1572872 | tf_op jit(solution)/shard_map/ppermute | solution.py:45
  663.6 27.2 %collective-permute-start.77 = (bf16[4,128,2048]{2,1,0:T(8,128)(2,1)S(1)}, bf16[4,128,2048]{2,1,0:T(8,128)(2,1)S(1)}, u32[]{:S(2)}, u32[]{:S(2)}) collective-permute-start(bf16[4,128,2048]{2,1,0:T(8,128)(2,1)S(1)} %get-tuple-element.309), channel_id=1, source_target_pairs={{0,1},{1,0},{2,3},{3,2},{4,5},{5,4},{6,7},{7,6},{8,9},{9,8},{10,11... | collective-permute-start | bytes 6291464 | tf_op jit(solution)/shard_map/ppermute | solution.py:45
  732.9 32.3 %collective-permute-start.106 = (bf16[512,768]{1,0:T(8,128)(2,1)S(1)}, bf16[512,768]{1,0:T(8,128)(2,1)S(1)}, u32[]{:S(2)}, u32[]{:S(2)}) collective-permute-start(bf16[512,768]{1,0:T(8,128)(2,1)S(1)} %get-tuple-element.301), channel_id=1, source_target_pairs={{0,4},{2,6},{4,0},{6,2},{1,5},{3,7},{5,1},{7,3},{8,12},{10,14},{12... | collective-permute-start | bytes 2359304 | tf_op jit(solution)/shard_map/ppermute | solution.py:45
  734.3 35.3 %collective-permute-start.110 = (bf16[512,768]{1,0:T(8,128)(2,1)S(1)}, bf16[512,768]{1,0:T(8,128)(2,1)S(1)}, u32[]{:S(2)}, u32[]{:S(2)}) collective-permute-start(bf16[512,768]{1,0:T(8,128)(2,1)S(1)} %get-tuple-element.300), channel_id=1, source_target_pairs={{0,6},{2,4},{4,2},{6,0},{1,7},{3,5},{5,3},{7,1},{8,14},{10,12},{12... | collective-permute-start | bytes 2359304 | tf_op jit(solution)/shard_map/ppermute | solution.py:45
  743.6 36.3 %collective-permute-start.121 = (bf16[512,512]{1,0:T(8,128)(2,1)S(1)}, bf16[512,512]{1,0:T(8,128)(2,1)S(1)}, u32[]{:S(2)}, u32[]{:S(2)}) collective-permute-start(bf16[512,512]{1,0:T(8,128)(2,1)S(1)} %get-tuple-element.306), channel_id=1, source_target_pairs={{0,2},{2,0},{4,6},{6,4},{1,3},{3,1},{5,7},{7,5},{8,10},{10,8},{12,... | collective-permute-start | bytes 1572872 | tf_op jit(solution)/shard_map/ppermute | solution.py:45
  749.9 37.1 %collective-permute-start.125 = (bf16[512,512]{1,0:T(8,128)(2,1)S(1)}, bf16[512,512]{1,0:T(8,128)(2,1)S(1)}, u32[]{:S(2)}, u32[]{:S(2)}) collective-permute-start(bf16[512,512]{1,0:T(8,128)(2,1)S(1)} %get-tuple-element.305), channel_id=1, source_target_pairs={{0,4},{2,6},{4,0},{6,2},{1,5},{3,7},{5,1},{7,3},{8,12},{10,14},{12... | collective-permute-start | bytes 1572872 | tf_op jit(solution)/shard_map/ppermute | solution.py:45
  751.9 35.1 %collective-permute-start.129 = (bf16[512,512]{1,0:T(8,128)(2,1)S(1)}, bf16[512,512]{1,0:T(8,128)(2,1)S(1)}, u32[]{:S(2)}, u32[]{:S(2)}) collective-permute-start(bf16[512,512]{1,0:T(8,128)(2,1)S(1)} %get-tuple-element.304), channel_id=1, source_target_pairs={{0,6},{2,4},{4,2},{6,0},{1,7},{3,5},{5,3},{7,1},{8,14},{10,12},{12... | collective-permute-start | bytes 1572872 | tf_op jit(solution)/shard_map/ppermute | solution.py:45
  780.0 218.7 %collective-permute-start.94 = (bf16[128,2048]{1,0:T(8,128)(2,1)}, bf16[128,2048]{1,0:T(8,128)(2,1)}, u32[]{:S(2)}, u32[]{:S(2)}) collective-permute-start(bf16[128,2048]{1,0:T(8,128)(2,1)} %add_convert_fusion.22), channel_id=1, source_target_pairs={{0,16},{8,24},{16,0},{24,8},{1,17},{9,25},{17,1},{25,9},{2,18},{10... | collective-permute-start | bytes 1572872 | tf_op jit(solution)/shard_map/ppermute | solution.py:45
  787.0 116.9 %collective-permute-start.78 = (bf16[4,128,2048]{2,1,0:T(8,128)(2,1)S(1)}, bf16[4,128,2048]{2,1,0:T(8,128)(2,1)S(1)}, u32[]{:S(2)}, u32[]{:S(2)}) collective-permute-start(bf16[4,128,2048]{2,1,0:T(8,128)(2,1)S(1)} %bitcast.254), channel_id=1, source_target_pairs={{0,1},{1,0},{2,3},{3,2},{4,5},{5,4},{6,7},{7,6},{8,9},{9,8},{10,11... | collective-permute-start | bytes 6291464 | tf_op jit(solution)/shard_map/ppermute | solution.py:45
  788.6 30.1 %collective-permute-start.130 = (bf16[512,512]{1,0:T(8,128)(2,1)S(1)}, bf16[512,512]{1,0:T(8,128)(2,1)S(1)}, u32[]{:S(2)}, u32[]{:S(2)}) collective-permute-start(bf16[512,512]{1,0:T(8,128)(2,1)S(1)} %collective-permute-done.129), channel_id=1, source_target_pairs={{0,8},{24,16},{1,9},{25,17},{2,10},{26,18},{3,11},{27,19},{4,12},{... | collective-permute-start | bytes 1572872 | tf_op jit(solution)/shard_map/ppermute | solution.py:485
  799.2 30.7 %collective-permute-start.103 = (bf16[512,512]{1,0:T(8,128)(2,1)S(1)}, bf16[512,512]{1,0:T(8,128)(2,1)S(1)}, u32[]{:S(2)}, u32[]{:S(2)}) collective-permute-start(bf16[512,512]{1,0:T(8,128)(2,1)S(1)} %slice.429), channel_id=1, source_target_pairs={{0,8},{24,16},{1,9},{25,17},{2,10},{26,18},{3,11},{27,19},{4,12},{... | collective-permute-start | bytes 1572872 | tf_op jit(solution)/shard_map/ppermute | solution.py:485
  807.4 33.7 %collective-permute-start.107 = (bf16[512,512]{1,0:T(8,128)(2,1)S(1)}, bf16[512,512]{1,0:T(8,128)(2,1)S(1)}, u32[]{:S(2)}, u32[]{:S(2)}) collective-permute-start(bf16[512,512]{1,0:T(8,128)(2,1)S(1)} %slice.430), channel_id=1, source_target_pairs={{0,8},{24,16},{1,9},{25,17},{2,10},{26,18},{3,11},{27,19},{4,12},{... | collective-permute-start | bytes 1572872 | tf_op jit(solution)/shard_map/ppermute | solution.py:485
  818.6 30.2 %collective-permute-start.111 = (bf16[512,512]{1,0:T(8,128)(2,1)S(1)}, bf16[512,512]{1,0:T(8,128)(2,1)S(1)}, u32[]{:S(2)}, u32[]{:S(2)}) collective-permute-start(bf16[512,512]{1,0:T(8,128)(2,1)S(1)} %slice.431), channel_id=1, source_target_pairs={{0,8},{24,16},{1,9},{25,17},{2,10},{26,18},{3,11},{27,19},{4,12},{... | collective-permute-start | bytes 1572872 | tf_op jit(solution)/shard_map/ppermute | solution.py:485
  852.0 25.0 %collective-permute-start.120 = (bf16[512,512]{1,0:T(8,128)(2,1)S(1)}, bf16[512,512]{1,0:T(8,128)(2,1)S(1)}, u32[]{:S(2)}, u32[]{:S(2)}) collective-permute-start(bf16[512,512]{1,0:T(8,128)(2,1)S(1)} %add_convert_fusion.6), channel_id=1, source_target_pairs={{8,0},{16,24},{9,1},{17,25},{10,2},{18,26},{11,3},{19,27},{12,4},{... | collective-permute-start | bytes 1572872 | tf_op jit(solution)/shard_map/ppermute | solution.py:488
  863.7 32.2 %collective-permute-start.108 = (bf16[512,512]{1,0:T(8,128)(2,1)S(1)}, bf16[512,512]{1,0:T(8,128)(2,1)S(1)}, u32[]{:S(2)}, u32[]{:S(2)}) collective-permute-start(bf16[512,512]{1,0:T(8,128)(2,1)S(1)} %add_convert_fusion.14), channel_id=1, source_target_pairs={{8,16},{16,8},{9,17},{17,9},{10,18},{18,10},{11,19},{19,11},{12,20... | collective-permute-start | bytes 1572872 | tf_op jit(solution)/shard_map/ppermute | solution.py:487
  897.4 29.8 %collective-permute-start.128 = (bf16[512,512]{1,0:T(8,128)(2,1)S(1)}, bf16[512,512]{1,0:T(8,128)(2,1)S(1)}, u32[]{:S(2)}, u32[]{:S(2)}) collective-permute-start(bf16[512,512]{1,0:T(8,128)(2,1)S(1)} %add_convert_fusion.2), channel_id=1, source_target_pairs={{8,0},{16,24},{9,1},{17,25},{10,2},{18,26},{11,3},{19,27},{12,4},{... | collective-permute-start | bytes 1572872 | tf_op jit(solution)/shard_map/ppermute | solution.py:488
  902.4 36.0 %collective-permute-start.132 = (bf16[512,512]{1,0:T(8,128)(2,1)S(1)}, bf16[512,512]{1,0:T(8,128)(2,1)S(1)}, u32[]{:S(2)}, u32[]{:S(2)}) collective-permute-start(bf16[512,512]{1,0:T(8,128)(2,1)S(1)} %add_convert_fusion), channel_id=1, source_target_pairs={{8,0},{16,24},{9,1},{17,25},{10,2},{18,26},{11,3},{19,27},{12,4},{... | collective-permute-start | bytes 1572872 | tf_op jit(solution)/shard_map/ppermute | solution.py:488
  903.8 55.9 %collective-permute-start.105 = (bf16[512,512]{1,0:T(8,128)(2,1)S(1)}, bf16[512,512]{1,0:T(8,128)(2,1)S(1)}, u32[]{:S(2)}, u32[]{:S(2)}) collective-permute-start(bf16[512,512]{1,0:T(8,128)(2,1)S(1)} %add_convert_fusion.15), channel_id=1, source_target_pairs={{8,0},{16,24},{9,1},{17,25},{10,2},{18,26},{11,3},{19,27},{12,4},{... | collective-permute-start | bytes 1572872 | tf_op jit(solution)/shard_map/ppermute | solution.py:488
  914.7 48.5 %collective-permute-start.109 = (bf16[512,512]{1,0:T(8,128)(2,1)S(1)}, bf16[512,512]{1,0:T(8,128)(2,1)S(1)}, u32[]{:S(2)}, u32[]{:S(2)}) collective-permute-start(bf16[512,512]{1,0:T(8,128)(2,1)S(1)} %add_convert_fusion.13), channel_id=1, source_target_pairs={{8,0},{16,24},{9,1},{17,25},{10,2},{18,26},{11,3},{19,27},{12,4},{... | collective-permute-start | bytes 1572872 | tf_op jit(solution)/shard_map/ppermute | solution.py:488
  927.2 44.9 %collective-permute-start.113 = (bf16[512,512]{1,0:T(8,128)(2,1)S(1)}, bf16[512,512]{1,0:T(8,128)(2,1)S(1)}, u32[]{:S(2)}, u32[]{:S(2)}) collective-permute-start(bf16[512,512]{1,0:T(8,128)(2,1)S(1)} %add_convert_fusion.11), channel_id=1, source_target_pairs={{8,0},{16,24},{9,1},{17,25},{10,2},{18,26},{11,3},{19,27},{12,4},{... | collective-permute-start | bytes 1572872 | tf_op jit(solution)/shard_map/ppermute | solution.py:488
  963.1 57.4 %collective-permute-start.117 = (bf16[512,512]{1,0:T(8,128)(2,1)}, bf16[512,512]{1,0:T(8,128)(2,1)}, u32[]{:S(2)}, u32[]{:S(2)}) collective-permute-start(bf16[512,512]{1,0:T(8,128)(2,1)} %add_convert_fusion.8), channel_id=1, source_target_pairs={{8,0},{16,24},{9,1},{17,25},{10,2},{18,26},{11,3},{19,27},{12,4},{... | collective-permute-start | bytes 1572872 | tf_op jit(solution)/shard_map/ppermute | solution.py:488
  974.8 38.5 %collective-permute-start.97 = (bf16[128,2048]{1,0:T(8,128)(2,1)}, bf16[128,2048]{1,0:T(8,128)(2,1)}, u32[]{:S(2)}, u32[]{:S(2)}) collective-permute-start(bf16[128,2048]{1,0:T(8,128)(2,1)} %get-tuple-element.207), channel_id=1, source_target_pairs={{0,4},{2,6},{4,0},{6,2},{1,5},{3,7},{5,1},{7,3},{8,12},{10,14},{12... | collective-permute-start | bytes 1572872 | tf_op jit(solution)/shard_map/ppermute | solution.py:45
  998.7 39.5 %collective-permute-start.83 = (bf16[128,2048]{1,0:T(8,128)(2,1)S(1)}, bf16[128,2048]{1,0:T(8,128)(2,1)}, u32[]{:S(2)}, u32[]{:S(2)}) collective-permute-start(bf16[128,2048]{1,0:T(8,128)(2,1)S(1)} %copy-done.32), channel_id=1, source_target_pairs={{0,2},{2,0},{4,6},{6,4},{1,3},{3,1},{5,7},{7,5},{8,10},{10,8},{12,... | collective-permute-start | bytes 1572872 | tf_op jit(solution)/shard_map/ppermute | solution.py:45
  1001.3 36.9 %collective-permute-start.85 = (bf16[128,2048]{1,0:T(8,128)(2,1)}, bf16[128,2048]{1,0:T(8,128)(2,1)}, u32[]{:S(2)}, u32[]{:S(2)}) collective-permute-start(bf16[128,2048]{1,0:T(8,128)(2,1)} %add_convert_fusion.26), channel_id=1, source_target_pairs={{0,4},{2,6},{4,0},{6,2},{1,5},{3,7},{5,1},{7,3},{8,12},{10,14},{12... | collective-permute-start | bytes 1572872 | tf_op jit(solution)/shard_map/ppermute | solution.py:45
  (165 other events, 2731.0 us)
where the time goes:
time: 1050 us; the launch traced here: 1040 us
  waiting for transfers between devices  471 us (45%)
  starting transfers between devices  215 us (20%)
  Pallas kernels  155 us (15%)
  local copies, waits for them, and re-layouts  90.5 us (9%)
  other arithmetic  61.2 us (6%)
  matrix products  46.1 us (4%)
    ppermute x106, waiting for transfers between devices, flip(): return lax.ppermute(values, axis, [(i, i ^ mask) for i in range(size)])  353 us
    ppermute x106, starting transfers between devices, flip(): return lax.ppermute(values, axis, [(i, i ^ mask) for i in range(size)])  124 us
    ppermute x9, waiting for transfers between devices, chain_tok(): outward = lax.ppermute(whole, 'tok', [(1, 0), (2, 3)])  54.6 us
    ppermute x9, waiting for transfers between devices, chain_tok(): inward = lax.ppermute(values, 'tok', [(0, 1), (3, 2)])  52.9 us
    ppermute x9, starting transfers between devices, chain_tok(): inward = lax.ppermute(values, 'tok', [(0, 1), (3, 2)])  48.6 us
    unnamed x192, local copies, waits for them, and re-layouts  47.3 us
    dot_general x13, matrix products, contract(): lax.dot_general(left, right, (dims, ((), ())), preferred_element_type=F32)  38.9 us
    pallas_call x4, Pallas kernels, expert(): pl.pallas_call(expert_kernel, grid=(count // tile,), in_specs=[spec(D), s...  33.7 us
  transfers between devices with their start and end apart: 138, of which 61 were waited for; matrix products, arithmetic and copies ran while one was open for 12% of the time, Pallas kernels for 13%

commit v1 on v0

--- a/solution.py
+++ b/solution.py
@@ -75,9 +75,9 @@
 
 
 def softmax_of(query_rows, key_rows, mask_ref):
-    scores = contract(query_rows, key_rows, ((1,), (1,))) * (1.0 / math.sqrt(HD))
-    raised = jnp.where(mask_ref[0] > 0.0, jnp.exp(scores), 0.0)
-    return raised / jnp.sum(raised, axis=-1, keepdims=True)
+    scores = contract(query_rows, key_rows, ((1,), (1,)))
+    raised = jnp.exp2(scores * (math.log2(math.e) / math.sqrt(HD))) * mask_ref[0]
+    return raised * (1.0 / jnp.sum(raised, axis=-1, keepdims=True))
 
 
 def key_parts(heads, raw_ref):
@@ -414,6 +414,32 @@
     )(*lefts, *rights)
 
 
+def kv_columns_kernel(heads_sm, *refs):
+    out_ref = refs[-1]
+    rows = out_ref.shape[0]
+    for side in range(2):
+        for head in range(KV):
+            acc = jnp.zeros((rows, HD), F32)
+            for m, ref in enumerate(refs[:-1]):
+                part = ref[:, side * HD : (side + 1) * HD].astype(F32)
+                acc = acc + jnp.where(heads_sm[m] == head, part, 0.0)
+            out_ref[:, (side * KV + head) * HD : (side * KV + head + 1) * HD] = acc
+
+
+def kv_columns(parts, kv_heads):
+    rows = parts[0].shape[0]
+    return pl.pallas_call(
+        kv_columns_kernel,
+        in_specs=[pl.BlockSpec(memory_space=pltpu.SMEM)]
+        + [pl.BlockSpec(memory_space=pltpu.VMEM)] * len(parts),
+        out_specs=pl.BlockSpec(memory_space=pltpu.VMEM),
+        out_shape=jax.ShapeDtypeStruct((rows, 2 * KV * HD), F32),
+        compiler_params=pltpu.CompilerParams(vmem_limit_bytes=16 << 20),
+        cost_estimate=estimate(1 << 20, *parts, *parts),
+        name="kvcols",
+    )(jnp.stack(kv_heads).astype(jnp.int32), *parts)
+
+
 def after(values, *others):
     return lax.optimization_barrier((values,) + others)[0]
 
@@ -486,7 +512,7 @@
         pair = lax.optimization_barrier(narrow(values, inward))
         whole = lax.optimization_barrier(narrow(pair, lax.ppermute(pair, "tok", [(1, 2), (2, 1)])))
         outward = lax.ppermute(whole, "tok", [(1, 0), (2, 3)])
-        return jnp.where(inner, whole, outward).astype(F32)
+        return jnp.where(inner, whole, outward).astype(F32), pair
 
     def sum_small(values):
         devices = nt * nr * nc
@@ -604,6 +630,10 @@
         sine = jnp.sin(angles)
         sine = jnp.concatenate([-sine, sine], axis=2)
 
+        plane_norm = after(jnp.stack(plane_norm), mask, cosine, sine)
+        normed_all = jnp.stack(cols_of(plane_norm)).reshape(nc * nr * tokens, D)
+        raw = matmul(normed_all, weight_qkv).reshape(nc, nr, tokens, all_cols)
+
         chosen = jnp.any(
             expert_ids[:, :, None] == jnp.arange(experts, dtype=jnp.int32)[None, None, :], axis=1
         )
@@ -615,26 +645,14 @@
         relative = jnp.arange(nt * nr, dtype=jnp.int32)
         block_order = ((relative // nr) ^ tok_i) * nr + ((relative % nr) ^ row_i)
 
-        def by_place(table):
-            sent = table.T.reshape(nt * nr, nc * tokens)
-            got = lax.all_to_all(sent, ("tok", "row"), 0, 0)
-            got = jnp.take(got, block_order, axis=0).reshape(nt, nr, nc, tokens)
-            return jnp.take(got, col_order, axis=2)
-
-        rank_rows = by_place(after(rank, *plane_norm))
-        rank_cols = rank_rows.transpose(0, 1, 3, 2)
-
-        normed_all = jnp.stack(cols_of(jnp.stack(plane_norm))).reshape(nc * nr * tokens, D)
-        raw = matmul(after(normed_all, mask, cosine, sine), weight_qkv).reshape(nc, nr, tokens, all_cols)
-
         cot_plane = plane_rows(cotangent)
-        cot_two = [tok(part, 2) for part in cot_plane]
-        cot_planes = {
-            0: cot_plane,
-            1: [tok(part, 1) for part in cot_plane],
-            2: cot_two,
-            3: [tok(part, 1) for part in cot_two],
-        }
+        cot_planes = {0: cot_plane}
+        for z in (1, 2, 3):
+            if z == 3:
+                first, last = (tok(cot_planes[2][k], 1) for k in (0, 3))
+            else:
+                first, last = (tok(cot_plane[k], z) for k in (0, 3))
+            cot_planes[z] = [first, row(first, 1), row(first, 2), last]
 
         qg, kg = query_gain[None], key_gain[None]
         mixed = attend(heads, raw, cosine, sine, mask, qg, kg)
@@ -661,8 +679,19 @@
         logits = matmul(normed2, router)
         raised = jnp.where(chosen, jnp.exp(logits), 0.0)
         gate = raised / jnp.sum(raised, axis=1, keepdims=True)
-        gate_rows = by_place(gate)
-        gate_cols = gate_rows.transpose(0, 1, 3, 2)
+        sent = jnp.concatenate(
+            [
+                rank.T.reshape(nt * nr, nc * tokens),
+                gate.T.reshape(nt * nr, nc * tokens),
+            ],
+            axis=1,
+        )
+        tables = lax.all_to_all(sent, ("tok", "row"), 0, 0)
+        tables = after(tables, row_planes[3][0])
+        tables = jnp.take(tables, block_order, axis=0).reshape(nt, nr, 2, nc, tokens)
+        tables = jnp.take(tables, col_order, axis=3)
+        rank_rows, gate_rows = tables[:, :, 0], tables[:, :, 1]
+        rank_cols, gate_cols = (t.transpose(0, 1, 3, 2) for t in (rank_rows, gate_rows))
 
         def of_planes(table, planes):
             return jnp.concatenate([table[z] for z in planes])
@@ -692,7 +721,7 @@
             picked = exchange(
                 pick(
                     after(
-                        tuple(block for z in planes for block in row_planes[z]), *hidden_grad[i]
+                        tuple(block for z in planes for block in row_planes[z]), *hidden_grad[0], *hidden_grad[1]
                     ),
                     of_planes(rank_rows, planes),
                     capacity,
@@ -762,12 +791,14 @@
         )
         output_part = contract(mixed.reshape(-1, head_cols), out_all, ((0,), (0,)))
         output_block = jnp.zeros((nr * head_cols, row_block), F32)
+        pairs = []
         for m in (0, 1, 2, 3):
             message = lax.dynamic_slice_in_dim(
                 output_part, (row_i ^ m) * row_block, row_block, 1
             ).astype(BF)
             message = row(message, m) if m else message
-            summed = chain_tok(message)
+            summed, pair = chain_tok(message)
+            pairs.append(pair)
             output_block = lax.dynamic_update_slice(
                 output_block, summed, ((row_i ^ m) * head_cols, 0)
             )
@@ -782,28 +813,25 @@
 
         qkv_part = contract(normed_all, qkv_send.reshape(-1, all_cols), ((0,), (0,)))
         query_block = jnp.zeros((row_block, nr * head_cols), F32)
-        full = jnp.zeros((row_block, 2 * key_cols), F32)
+        messages = []
         for m in (0, 1, 2, 3):
             message = lax.dynamic_slice_in_dim(
                 qkv_part, (row_i ^ m) * row_block, row_block, 0
             ).astype(BF)
-            message = row(message, m) if m else message
-            summed = chain_tok(message[:, :head_cols])
+            if m:
+                message = after(row(message, m), pairs[min(m + 1, 3)])
+            messages.append(message)
+            summed, _ = chain_tok(message[:, :head_cols])
             query_block = lax.dynamic_update_slice(
                 query_block, summed, (0, (row_i ^ m) * head_cols)
             )
-            for half in range(2):
-                start = half * key_cols + kv_heads[m] * HD
-                first = head_cols + half * HD
-                now = lax.dynamic_slice(full, (0, start), (row_block, HD))
-                new = now + message[:, first : first + HD].astype(F32)
-                full = lax.dynamic_update_slice(full, new, (0, start))
+        full = kv_columns([message[:, head_cols:] for message in messages], kv_heads)
         pieces = [
             lax.dynamic_slice(full, (0, (col_i ^ m) * width), (row_block, width))
             for m in range(nc)
         ]
         keyval_mine = narrow(pieces[0], *[col(pieces[m].astype(BF), m) for m in range(1, nc)])
-        keyval_block = chain_tok(keyval_mine)
+        keyval_block, _ = chain_tok(keyval_mine)
 
         mix_three = narrow(*reduce_plane(mix[0][4:], True))
         mix_two = narrow(*reduce_plane(mix[0][:4], False), tok(mix_three, 1))

time: 1050 us -> 981 us (0.934)
  waiting for transfers between devices: 471 us -> 378 us
  starting transfers between devices: 215 us -> 246 us
    ppermute x106, waiting for transfers between devices: 353 us -> 290 us  [flip(): return lax.ppermute(values, axis, [(i, i ^ mask) for i in range(size)])]
    ppermute x9, starting transfers between devices: 48.6 us -> 99.4 us  [chain_tok(): inward = lax.ppermute(values, 'tok', [(0, 1), (3, 2)])]
    ppermute x9, waiting for transfers between devices: 52.9 us -> 24.2 us  [chain_tok(): inward = lax.ppermute(values, 'tok', [(0, 1), (3, 2)])]
    ppermute x9, waiting for transfers between devices: 54.6 us -> 42 us  [chain_tok(): outward = lax.ppermute(whole, 'tok', [(1, 0), (2, 3)])]
    ppermute x106, starting transfers between devices: 124 us -> 113 us  [flip(): return lax.ppermute(values, axis, [(i, i ^ mask) for i in range(size)])]
    all_to_all x2 -> x1, waiting for transfers between devices: 1.86 us -> 12.5 us  [layer(): tables = lax.all_to_all(sent, ('tok', 'row'), 0, 0)]
    unnamed x192 -> x246, local copies, waits for them, and re-layouts: 47.3 us -> 52.3 us
  transfers between devices with their start and end apart: 138 -> 137, of which waited for: 61 -> 49; matrix products, arithmetic and copies ran while one was open for 12% -> 12% of each run, Pallas kernels for 13% -> 14%
where the time goes in v1:
time: 981 us; the launch traced here: 971 us
  waiting for transfers between devices  378 us (39%)
  starting transfers between devices  246 us (25%)
  Pallas kernels  156 us (16%)
  local copies, waits for them, and re-layouts  88.4 us (9%)
  other arithmetic  52.8 us (5%)
  matrix products  46.2 us (5%)
    ppermute x106, waiting for transfers between devices, flip(): return lax.ppermute(values, axis, [(i, i ^ mask) for i in range(size)])  290 us
    ppermute x106, starting transfers between devices, flip(): return lax.ppermute(values, axis, [(i, i ^ mask) for i in range(size)])  113 us
    ppermute x9, starting transfers between devices, chain_tok(): inward = lax.ppermute(values, 'tok', [(0, 1), (3, 2)])  99.4 us
    unnamed x246, local copies, waits for them, and re-layouts  52.3 us
    ppermute x9, waiting for transfers between devices, chain_tok(): outward = lax.ppermute(whole, 'tok', [(1, 0), (2, 3)])  42 us
    dot_general x13, matrix products, contract(): lax.dot_general(left, right, (dims, ((), ())), preferred_element_type=F32)  36.9 us
    pallas_call x4, Pallas kernels, expert(): pl.pallas_call(expert_kernel, grid=(count // tile,), in_specs=[spec(D), s...  33.6 us
    pallas_call x2, Pallas kernels, weight_grad(): pl.pallas_call(functools.partial(weight_grad_kernel, count), grid=(m // t...  29.3 us
  transfers between devices with their start and end apart: 137, of which 49 were waited for; matrix products, arithmetic and copies ran while one was open for 12% of the time, Pallas kernels for 14%

profile of v1, /device:TPU:0, one launch (start us, length us, event | category | flops | bytes accessed | tf_op | source)
XLA Modules:
  0.0 970.9 jit_solution(2462682254397723045)
XLA Ops:
  1.4 3.9 collective-permute-start.6
  17.4 4.2 collective-permute-done
  40.6 15.0 %collective-permute-done.9 = bf16[512,768]{1,0:T(8,128)(2,1)S(1)} collective-permute-done((bf16[512,768]{1,0:T(8,128)(2,1)S(1)}, bf16[512,768]{1,0:T(8,128)(2,1)S(1)}, u32[]{:S(2)}, u32[]{:S(2)}) %collective-permute-start.9) | collective-permute-done | bytes 786464 | tf_op jit(solution)/shard_map/ppermute | solution.py:45
  57.3 15.1 %collective-permute-done.10 = bf16[512,768]{1,0:T(8,128)(2,1)S(1)} collective-permute-done((bf16[512,768]{1,0:T(8,128)(2,1)S(1)}, bf16[512,768]{1,0:T(8,128)(2,1)S(1)}, u32[]{:S(2)}, u32[]{:S(2)}) %collective-permute-start.10) | collective-permute-done | bytes 786464 | tf_op jit(solution)/shard_map/ppermute | solution.py:45
  74.1 7.8 fusion.raw_ref
  81.9 11.7 %attend.1.mixed_ref = bf16[2,4,128,512]{3,2,1,0:T(8,128)(2,1)} custom-call(f32[2,4,128,768]{3,2,1,0:T(8,128)} %fusion.raw_ref, f32[4,256,128]{2,1,0:T(8,128)} %get-tuple-element.364.cos_ref, f32[4,256,128]{2,1,0:T(8,128)} %get-tuple-element.365.sin_ref, f32[4,256,256]{2,1,0:T(8,128)} %and_convert_fusion.mask_ref, f32[1,128]{1,0:T(1,128)} %bitcast.253, ...), custom_call_target="tpu_custom_call" | custom-call | flops 4294967296 | bytes 4194304 | tf_op jit(solution)/shard_map/attend/pallas_call | solution.py:185
  115.4 14.2 %collective-permute-done.16 = bf16[64,2048]{1,0:T(8,128)(2,1)S(1)} collective-permute-done((bf16[64,2048]{1,0:T(8,128)(2,1)S(1)}, bf16[64,2048]{1,0:T(8,128)(2,1)S(1)}, u32[]{:S(2)}, u32[]{:S(2)}) %collective-permute-start.16) | collective-permute-done | bytes 262176 | tf_op jit(solution)/shard_map/ppermute | solution.py:45
  134.9 4.3 collective-permute-done.19
  149.7 15.5 %collective-permute-done.31.refs_0_ = bf16[128,2048]{1,0:T(8,128)(2,1)S(1)} collective-permute-done((bf16[128,2048]{1,0:T(8,128)(2,1)S(1)}, bf16[128,2048]{1,0:T(8,128)(2,1)S(1)}, u32[]{:S(2)}, u32[]{:S(2)}) %collective-permute-start.31) | collective-permute-done | bytes 524320 | tf_op jit(solution)/shard_map/ppermute | solution.py:45
  169.8 6.7 collective-permute-done.23.refs_0_
  179.9 5.9 all-to-all-start
  188.0 12.5 %all-to-all-done = f32[16,1,512]{2,1,0:T(1,128)} async-done(((f32[16,1,512]{2,1,0:T(1,128)}), f32[16,1,512]{2,1,0:T(1,128)}, u32[]{:S(2)}, u32[]{:S(2)}) %all-to-all-start) | async-done | bytes 32800 | tf_op jit(solution)/shard_map/all_to_all | solution.py:689
  212.3 14.7 %collective-permute-done.38.refs_3_ = bf16[128,2048]{1,0:T(8,128)(2,1)} collective-permute-done((bf16[128,2048]{1,0:T(8,128)(2,1)S(1)}, bf16[128,2048]{1,0:T(8,128)(2,1)}, u32[]{:S(2)}, u32[]{:S(2)}) %collective-permute-start.38) | collective-permute-done | bytes 524320 | tf_op jit(solution)/shard_map/ppermute | solution.py:45
  227.1 6.1 shard_map.230
  235.5 5.6 collective-permute-done.42.refs_7_
  243.2 6.4 shard_map.229
  252.2 4.7 fusion.66.d_ref
  260.0 4.5 collective-permute-done.24.refs_4_
  268.5 4.6 fusion.64.d_ref
  282.4 8.2 collective-permute-done.57.refs_6_
  290.6 9.9 %collective-permute-done.58.refs_7_ = bf16[128,2048]{1,0:T(8,128)(2,1)S(1)} collective-permute-done((bf16[128,2048]{1,0:T(8,128)(2,1)S(1)}, bf16[128,2048]{1,0:T(8,128)(2,1)S(1)}, u32[]{:S(2)}, u32[]{:S(2)}) %collective-permute-start.58) | collective-permute-done | bytes 524320 | tf_op jit(solution)/shard_map/ppermute | solution.py:45
  300.6 5.5 shard_map.238
  313.2 9.0 collective-permute-done.29.refs_6_
  322.2 10.8 %collective-permute-done.30.refs_7_ = bf16[128,2048]{1,0:T(8,128)(2,1)} collective-permute-done((bf16[128,2048]{1,0:T(8,128)(2,1)}, bf16[128,2048]{1,0:T(8,128)(2,1)}, u32[]{:S(2)}, u32[]{:S(2)}) %collective-permute-start.30) | collective-permute-done | bytes 524320 | tf_op jit(solution)/shard_map/ppermute | solution.py:45
  333.0 6.6 shard_map.231
  343.8 7.3 shard_map.239
  357.3 7.2 shard_map.232
  372.2 9.4 shard_map.240
  397.9 9.7 %shard_map.233 = (bf16[512,768]{1,0:T(8,128)(2,1)S(1)}, bf16[512,1536]{1,0:T(8,128)(2,1)S(1)}, bf16[512,2048]{1,0:T(8,128)(2,1)}) custom-call(bf16[512,2048]{1,0:T(8,128)(2,1)} %collective-permute-done.49.x_ref.refs_3_, f32[512,768]{1,0:T(8,128)S(1)} %copy-done.53, bf16[2048,1536]{1,0:T(8,128)(2,1)S(1)} %bitcast.226), custom_call_target="tpu_custom_call" | custom-call | flops 6442450944 | bytes 9961472 | tf_op jit(solution)/shard_map/pallas_call | solution.py:350
  408.1 4.8 shard_map.235
  426.1 7.1 shard_map.241
  435.8 17.7 %shard_map.245 = f32[2048,1536]{1,0:T(8,128)} custom-call(bf16[512,2048]{1,0:T(8,128)(2,1)} %get-tuple-element.158.x_ref.refs_0_, bf16[512,2048]{1,0:T(8,128)(2,1)} %collective-permute-done.59.x_ref.refs_1_, bf16[512,2048]{1,0:T(8,128)(2,1)} %get-tuple-element.135.x_ref.refs_2_, bf16[512,2048]{1,0:T(8,128)(2,1)} %collective-permute-done.49.x_ref.refs_3_, ...), custom_call_target="tpu_custom_call" | custom-call | flops 12884901888 | bytes 20971520 | tf_op jit(solution)/shard_map/pallas_call | solution.py:405
  456.0 5.9 shard_map.237
  465.3 3.7 collective-permute-done.62
  470.5 9.7 collective-permute-done.69
  481.4 10.0 %collective-permute-done.65 = bf16[128,2048]{1,0:T(8,128)(2,1)S(1)} collective-permute-done((bf16[128,2048]{1,0:T(8,128)(2,1)S(1)}, bf16[128,2048]{1,0:T(8,128)(2,1)S(1)}, u32[]{:S(2)}, u32[]{:S(2)}) %collective-permute-start.65) | collective-permute-done | bytes 524320 | tf_op jit(solution)/shard_map/ppermute | solution.py:45
  495.4 17.4 %collective-permute-done.70 = bf16[128,2048]{1,0:T(8,128)(2,1)S(1)} collective-permute-done((bf16[128,2048]{1,0:T(8,128)(2,1)S(1)}, bf16[128,2048]{1,0:T(8,128)(2,1)S(1)}, u32[]{:S(2)}, u32[]{:S(2)}) %collective-permute-start.70) | collective-permute-done | bytes 524320 | tf_op jit(solution)/shard_map/ppermute | solution.py:45
  519.9 7.4 shard_map.244
  529.7 8.3 collective-permute-done.72
  545.0 11.6 %shard_map.246 = f32[768,2048]{1,0:T(8,128)} custom-call(bf16[512,768]{1,0:T(8,128)(2,1)S(1)} %copy-done.22, bf16[512,768]{1,0:T(8,128)(2,1)S(1)} %copy-done.27, bf16[512,768]{1,0:T(8,128)(2,1)S(1)} %copy-done.25, bf16[512,768]{1,0:T(8,128)(2,1)S(1)} %copy-done.29, bf16[512,2048]{1,0:T(8,128)(2,1)S(1)} %copy-done.11, bf16[512,2048]{1,0:T(8,128)(2,1)} %copy-done.12, ...), custom_call_target="tpu_custom_call" | custom-call | flops 6442450944 | bytes 19922944 | tf_op jit(solution)/shard_map/pallas_call | solution.py:405
  567.9 20.5 %collective-permute-done.75 = bf16[64,2048]{1,0:T(8,128)(2,1)S(1)} collective-permute-done((bf16[64,2048]{1,0:T(8,128)(2,1)S(1)}, bf16[64,2048]{1,0:T(8,128)(2,1)S(1)}, u32[]{:S(2)}, u32[]{:S(2)}) %collective-permute-start.75) | collective-permute-done | bytes 262176 | tf_op jit(solution)/shard_map/ppermute | solution.py:45
  593.4 7.9 collective-permute-done.92
  604.7 7.0 shard_map.236
  625.0 15.8 %attend_back.1 = (bf16[2,4,128,768]{3,2,1,0:T(8,128)(2,1)}, f32[1,128]{1,0:T(1,128)}, f32[1,128]{1,0:T(1,128)}) custom-call(f32[2,4,128,768]{3,2,1,0:T(8,128)} %fusion.raw_ref, f32[4,256,128]{2,1,0:T(8,128)} %get-tuple-element.364.cos_ref, f32[4,256,128]{2,1,0:T(8,128)} %get-tuple-element.365.sin_ref, f32[4,256,256]{2,1,0:T(8,128)} %and_convert_fusion.mask_ref, ...), custom_call_target="tpu_custom_call" | custom-call | flops 6442450944 | bytes 7340032 | tf_op jit(solution)/shard_map/attend_back/pallas_call | solution.py:198
  640.8 5.6 convolution_bitcast_fusion
  661.2 5.3 collective-permute-done.125
  666.5 10.7 %collective-permute-done.109 = bf16[512,512]{1,0:T(8,128)(2,1)S(1)} collective-permute-done((bf16[512,512]{1,0:T(8,128)(2,1)S(1)}, bf16[512,512]{1,0:T(8,128)(2,1)S(1)}, u32[]{:S(2)}, u32[]{:S(2)}) %collective-permute-start.109) | collective-permute-done | bytes 524320 | tf_op jit(solution)/shard_map/ppermute | solution.py:45
  678.6 11.5 %collective-permute-done.103 = bf16[512,512]{1,0:T(8,128)(2,1)S(1)} collective-permute-done((bf16[512,512]{1,0:T(8,128)(2,1)S(1)}, bf16[512,512]{1,0:T(8,128)(2,1)S(1)}, u32[]{:S(2)}, u32[]{:S(2)}) %collective-permute-start.103) | collective-permute-done | bytes 524320 | tf_op jit(solution)/shard_map/ppermute | solution.py:45
  695.7 8.0 collective-permute-done.108
  711.4 51.4 %collective-permute-start.115 = (bf16[512,512]{1,0:T(8,128)(2,1)S(1)}, bf16[512,512]{1,0:T(8,128)(2,1)S(1)}, u32[]{:S(2)}, u32[]{:S(2)}) collective-permute-start(bf16[512,512]{1,0:T(8,128)(2,1)S(1)} %slice.359), channel_id=1, source_target_pairs={{0,8},{24,16},{1,9},{25,17},{2,10},{26,18},{3,11},{27,19},{4,12},{... | collective-permute-start | bytes 1572872 | tf_op jit(solution)/shard_map/ppermute | solution.py:511
  763.0 9.1 collective-permute-start.111
  774.8 4.7 collective-permute-start.105
  779.6 6.4 collective-permute-done.111
  786.2 9.6 collective-permute-done.105
  800.7 11.8 %collective-permute-done.124 = bf16[512,512]{1,0:T(8,128)(2,1)S(1)} collective-permute-done((bf16[512,512]{1,0:T(8,128)(2,1)S(1)}, bf16[512,512]{1,0:T(8,128)(2,1)S(1)}, u32[]{:S(2)}, u32[]{:S(2)}) %collective-permute-start.124) | collective-permute-done | bytes 524320 | tf_op jit(solution)/shard_map/ppermute | solution.py:514
  816.2 25.7 %collective-permute-start.119 = (bf16[512,512]{1,0:T(8,128)(2,1)S(1)}, bf16[512,512]{1,0:T(8,128)(2,1)S(1)}, u32[]{:S(2)}, u32[]{:S(2)}) collective-permute-start(bf16[512,512]{1,0:T(8,128)(2,1)S(1)} %add_convert_fusion.8), channel_id=1, source_target_pairs={{0,8},{24,16},{1,9},{25,17},{2,10},{26,18},{3,11},{27,19},{4,12},{... | collective-permute-start | bytes 1572872 | tf_op jit(solution)/shard_map/ppermute | solution.py:511
  843.5 5.1 collective-permute-done.119
  850.3 5.5 collective-permute-done.130
  863.3 24.7 %collective-permute-done.107 = bf16[512,512]{1,0:T(8,128)(2,1)S(1)} collective-permute-done((bf16[512,512]{1,0:T(8,128)(2,1)S(1)}, bf16[512,512]{1,0:T(8,128)(2,1)S(1)}, u32[]{:S(2)}, u32[]{:S(2)}) %collective-permute-start.107) | collective-permute-done | bytes 524320 | tf_op jit(solution)/shard_map/ppermute | solution.py:514
  893.0 5.1 collective-permute-done.80
  906.8 3.9 all-to-all-start.2
  918.0 10.3 %collective-permute-done.84 = bf16[128,2048]{1,0:T(8,128)(2,1)S(1)} collective-permute-done((bf16[128,2048]{1,0:T(8,128)(2,1)}, bf16[128,2048]{1,0:T(8,128)(2,1)S(1)}, u32[]{:S(2)}, u32[]{:S(2)}) %collective-permute-start.84) | collective-permute-done | bytes 524320 | tf_op jit(solution)/shard_map/ppermute | solution.py:45
  945.2 9.2 all-to-all-done.3
  966.3 4.2 fusion.9
  (700 shorter events, 337.2 us)
Async XLA Ops:
  31.4 42.8 %collective-permute-start.7 = (bf16[4,128,2048]{2,1,0:T(8,128)(2,1)S(1)}, bf16[4,128,2048]{2,1,0:T(8,128)(2,1)}, u32[]{:S(2)}, u32[]{:S(2)}) collective-permute-start(bf16[4,128,2048]{2,1,0:T(8,128)(2,1)S(1)} %pad_maximum_fusion.4), channel_id=1, source_target_pairs={{0,1},{1,0},{2,3},{3,2},{4,5},{5,4},{6,7},{7,6},{8,9},{9,8},{10,11... | collective-permute-start | bytes 6291464 | tf_op jit(solution)/shard_map/ppermute | solution.py:45
  35.9 36.5 %collective-permute-start.10 = (bf16[512,768]{1,0:T(8,128)(2,1)S(1)}, bf16[512,768]{1,0:T(8,128)(2,1)S(1)}, u32[]{:S(2)}, u32[]{:S(2)}) collective-permute-start(bf16[512,768]{1,0:T(8,128)(2,1)S(1)} %pad_maximum_fusion.7), channel_id=1, source_target_pairs={{0,2},{2,0},{4,6},{6,4},{1,3},{3,1},{5,7},{7,5},{8,10},{10,8},{12,... | collective-permute-start | bytes 2359304 | tf_op jit(solution)/shard_map/ppermute | solution.py:45
  37.6 36.4 %collective-permute-start.11 = (bf16[512,768]{1,0:T(8,128)(2,1)S(1)}, bf16[512,768]{1,0:T(8,128)(2,1)S(1)}, u32[]{:S(2)}, u32[]{:S(2)}) collective-permute-start(bf16[512,768]{1,0:T(8,128)(2,1)S(1)} %pad_maximum_fusion.8), channel_id=1, source_target_pairs={{0,4},{2,6},{4,0},{6,2},{1,5},{3,7},{5,1},{7,3},{8,12},{10,14},{12... | collective-permute-start | bytes 2359304 | tf_op jit(solution)/shard_map/ppermute | solution.py:45
  39.1 54.6 %collective-permute-start.14 = (bf16[512,512]{1,0:T(8,128)(2,1)}, bf16[512,512]{1,0:T(8,128)(2,1)}, u32[]{:S(2)}, u32[]{:S(2)}) collective-permute-start(bf16[512,512]{1,0:T(8,128)(2,1)} %get-tuple-element.312), channel_id=1, source_target_pairs={{0,4},{2,6},{4,0},{6,2},{1,5},{3,7},{5,1},{7,3},{8,12},{10,14},{12... | collective-permute-start | bytes 1572872 | tf_op jit(solution)/shard_map/ppermute | solution.py:45
  55.5 38.1 %collective-permute-start.13 = (bf16[512,512]{1,0:T(8,128)(2,1)S(1)}, bf16[512,512]{1,0:T(8,128)(2,1)}, u32[]{:S(2)}, u32[]{:S(2)}) collective-permute-start(bf16[512,512]{1,0:T(8,128)(2,1)S(1)} %get-tuple-element.313), channel_id=1, source_target_pairs={{0,2},{2,0},{4,6},{6,4},{1,3},{3,1},{5,7},{7,5},{8,10},{10,8},{12,... | collective-permute-start | bytes 1572872 | tf_op jit(solution)/shard_map/ppermute | solution.py:45
  106.1 42.4 %collective-permute-start.44 = (bf16[128,2048]{1,0:T(8,128)(2,1)S(1)}, bf16[128,2048]{1,0:T(8,128)(2,1)}, u32[]{:S(2)}, u32[]{:S(2)}) collective-permute-start(bf16[128,2048]{1,0:T(8,128)(2,1)S(1)} %copy-done.6), channel_id=1, source_target_pairs={{0,8},{8,0},{16,24},{24,16},{1,9},{9,1},{17,25},{25,17},{2,10},{10... | collective-permute-start | bytes 1572872 | tf_op jit(solution)/shard_map/ppermute | solution.py:45
  107.7 39.3 %collective-permute-start.36 = (bf16[128,2048]{1,0:T(8,128)(2,1)S(1)}, bf16[128,2048]{1,0:T(8,128)(2,1)S(1)}, u32[]{:S(2)}, u32[]{:S(2)}) collective-permute-start(bf16[128,2048]{1,0:T(8,128)(2,1)S(1)} %copy-done.6), channel_id=1, source_target_pairs={{0,2},{2,0},{4,6},{6,4},{1,3},{3,1},{5,7},{7,5},{8,10},{10,8},{12,... | collective-permute-start | bytes 1572872 | tf_op jit(solution)/shard_map/ppermute | solution.py:45
  131.6 33.7 %collective-permute-start.31 = (bf16[128,2048]{1,0:T(8,128)(2,1)S(1)}, bf16[128,2048]{1,0:T(8,128)(2,1)S(1)}, u32[]{:S(2)}, u32[]{:S(2)}) collective-permute-start(bf16[128,2048]{1,0:T(8,128)(2,1)S(1)} %copy-done.6), channel_id=1, source_target_pairs={{0,16},{8,24},{16,0},{24,8},{1,17},{9,25},{17,1},{25,9},{2,18},{10... | collective-permute-start | bytes 1572872 | tf_op jit(solution)/shard_map/ppermute | solution.py:45
  139.2 27.5 %collective-permute-start.35 = (bf16[64,2048]{1,0:T(8,128)(2,1)}, bf16[64,2048]{1,0:T(8,128)(2,1)}, u32[]{:S(2)}, u32[]{:S(2)}) collective-permute-start(bf16[64,2048]{1,0:T(8,128)(2,1)} %slice.398), channel_id=1, source_target_pairs={{0,2},{2,0},{4,6},{6,4},{1,3},{3,1},{5,7},{7,5},{8,10},{10,8},{12,... | collective-permute-start | bytes 786440 | tf_op jit(solution)/shard_map/ppermute | solution.py:45
  143.2 33.4 %collective-permute-start.23 = (bf16[128,2048]{1,0:T(8,128)(2,1)}, bf16[128,2048]{1,0:T(8,128)(2,1)}, u32[]{:S(2)}, u32[]{:S(2)}) collective-permute-start(bf16[128,2048]{1,0:T(8,128)(2,1)} %multiply_convert_fusion.refs_0_), channel_id=1, source_target_pairs={{0,16},{8,24},{16,0},{24,8},{1,17},{9,25},{17,1},{25,9},{2,18},{10... | collective-permute-start | bytes 1572872 | tf_op jit(solution)/shard_map/ppermute | solution.py:45
  147.7 38.1 %collective-permute-start.37 = (bf16[64,2048]{1,0:T(8,128)(2,1)}, bf16[64,2048]{1,0:T(8,128)(2,1)S(1)}, u32[]{:S(2)}, u32[]{:S(2)}) collective-permute-start(bf16[64,2048]{1,0:T(8,128)(2,1)} %slice.399), channel_id=1, source_target_pairs={{0,4},{2,6},{4,0},{6,2},{1,5},{3,7},{5,1},{7,3},{8,12},{10,14},{12... | collective-permute-start | bytes 786440 | tf_op jit(solution)/shard_map/ppermute | solution.py:45
  148.6 55.5 %collective-permute-start.46 = (bf16[128,2048]{1,0:T(8,128)(2,1)}, bf16[128,2048]{1,0:T(8,128)(2,1)}, u32[]{:S(2)}, u32[]{:S(2)}) collective-permute-start(bf16[128,2048]{1,0:T(8,128)(2,1)} %collective-permute-done.44.refs_4_), channel_id=1, source_target_pairs={{0,4},{2,6},{4,0},{6,2},{1,5},{3,7},{5,1},{7,3},{8,12},{10,14},{12... | collective-permute-start | bytes 1572872 | tf_op jit(solution)/shard_map/ppermute | solution.py:45
  165.2 40.5 %collective-permute-start.45 = (bf16[128,2048]{1,0:T(8,128)(2,1)}, bf16[128,2048]{1,0:T(8,128)(2,1)}, u32[]{:S(2)}, u32[]{:S(2)}) collective-permute-start(bf16[128,2048]{1,0:T(8,128)(2,1)} %collective-permute-done.44.refs_4_), channel_id=1, source_target_pairs={{0,2},{2,0},{4,6},{6,4},{1,3},{3,1},{5,7},{7,5},{8,10},{10,8},{12,... | collective-permute-start | bytes 1572872 | tf_op jit(solution)/shard_map/ppermute | solution.py:45
  166.7 39.6 %collective-permute-start.39 = (bf16[128,2048]{1,0:T(8,128)(2,1)S(1)}, bf16[128,2048]{1,0:T(8,128)(2,1)}, u32[]{:S(2)}, u32[]{:S(2)}) collective-permute-start(bf16[128,2048]{1,0:T(8,128)(2,1)S(1)} %collective-permute-done.31.refs_0_), channel_id=1, source_target_pairs={{0,8},{8,0},{16,24},{24,16},{1,9},{9,1},{17,25},{25,17},{2,10},{10... | collective-permute-start | bytes 1572872 | tf_op jit(solution)/shard_map/ppermute | solution.py:45
  176.6 24.6 %collective-permute-start.25 = (bf16[128,2048]{1,0:T(8,128)(2,1)}, bf16[128,2048]{1,0:T(8,128)(2,1)S(1)}, u32[]{:S(2)}, u32[]{:S(2)}) collective-permute-start(bf16[128,2048]{1,0:T(8,128)(2,1)} %collective-permute-done.23.refs_0_), channel_id=1, source_target_pairs={{0,8},{8,0},{16,24},{24,16},{1,9},{9,1},{17,25},{25,17},{2,10},{10... | collective-permute-start | bytes 1572872 | tf_op jit(solution)/shard_map/ppermute | solution.py:45
  185.9 25.0 %collective-permute-start.47 = (bf16[128,2048]{1,0:T(8,128)(2,1)S(1)}, bf16[128,2048]{1,0:T(8,128)(2,1)}, u32[]{:S(2)}, u32[]{:S(2)}) collective-permute-start(bf16[128,2048]{1,0:T(8,128)(2,1)S(1)} %constant_dynamic-update-slice_fusion.6.refs_3_), channel_id=1, source_target_pairs={{0,8},{8,0},{16,24},{24,16},{1,9},{9,1},{17,25},{25,17},{2,10},{10... | collective-permute-start | bytes 1572872 | tf_op jit(solution)/shard_map/ppermute | solution.py:45
  201.2 25.9 %collective-permute-start.38 = (bf16[128,2048]{1,0:T(8,128)(2,1)S(1)}, bf16[128,2048]{1,0:T(8,128)(2,1)}, u32[]{:S(2)}, u32[]{:S(2)}) collective-permute-start(bf16[128,2048]{1,0:T(8,128)(2,1)S(1)} %constant_dynamic-update-slice_fusion.6.refs_3_), channel_id=1, source_target_pairs={{0,16},{8,24},{16,0},{24,8},{1,17},{9,25},{17,1},{25,9},{2,18},{10... | collective-permute-start | bytes 1572872 | tf_op jit(solution)/shard_map/ppermute | solution.py:45
  204.1 29.2 %collective-permute-start.33 = (bf16[128,2048]{1,0:T(8,128)(2,1)S(1)}, bf16[128,2048]{1,0:T(8,128)(2,1)S(1)}, u32[]{:S(2)}, u32[]{:S(2)}) collective-permute-start(bf16[128,2048]{1,0:T(8,128)(2,1)S(1)} %collective-permute-done.31.refs_0_), channel_id=1, source_target_pairs={{0,4},{2,6},{4,0},{6,2},{1,5},{3,7},{5,1},{7,3},{8,12},{10,14},{12... | collective-permute-start | bytes 1572872 | tf_op jit(solution)/shard_map/ppermute | solution.py:45
  205.7 28.6 %collective-permute-start.32 = (bf16[128,2048]{1,0:T(8,128)(2,1)S(1)}, bf16[128,2048]{1,0:T(8,128)(2,1)}, u32[]{:S(2)}, u32[]{:S(2)}) collective-permute-start(bf16[128,2048]{1,0:T(8,128)(2,1)S(1)} %collective-permute-done.31.refs_0_), channel_id=1, source_target_pairs={{0,2},{2,0},{4,6},{6,4},{1,3},{3,1},{5,7},{7,5},{8,10},{10,8},{12,... | collective-permute-start | bytes 1572872 | tf_op jit(solution)/shard_map/ppermute | solution.py:45
  206.3 29.1 %collective-permute-start.41 = (bf16[128,2048]{1,0:T(8,128)(2,1)}, bf16[128,2048]{1,0:T(8,128)(2,1)}, u32[]{:S(2)}, u32[]{:S(2)}) collective-permute-start(bf16[128,2048]{1,0:T(8,128)(2,1)} %collective-permute-done.39.refs_4_), channel_id=1, source_target_pairs={{0,4},{2,6},{4,0},{6,2},{1,5},{3,7},{5,1},{7,3},{8,12},{10,14},{12... | collective-permute-start | bytes 1572872 | tf_op jit(solution)/shard_map/ppermute | solution.py:45
  234.1 33.6 %collective-permute-start.48 = (bf16[512,2048]{1,0:T(8,128)(2,1)}, bf16[512,2048]{1,0:T(8,128)(2,1)}, u32[]{:S(2)}, u32[]{:S(2)}) collective-permute-start(bf16[512,2048]{1,0:T(8,128)(2,1)} %get-tuple-element.126), channel_id=1, source_target_pairs={{0,1},{1,0},{2,3},{3,2},{4,5},{5,4},{6,7},{7,6},{8,9},{9,8},{10,11... | collective-permute-start | bytes 6291464 | tf_op jit(solution)/shard_map/ppermute | solution.py:45
  265.6 25.0 %collective-permute-start.57 = (bf16[128,2048]{1,0:T(8,128)(2,1)S(1)}, bf16[128,2048]{1,0:T(8,128)(2,1)S(1)}, u32[]{:S(2)}, u32[]{:S(2)}) collective-permute-start(bf16[128,2048]{1,0:T(8,128)(2,1)S(1)} %copy-done.35), channel_id=1, source_target_pairs={{0,4},{2,6},{4,0},{6,2},{1,5},{3,7},{5,1},{7,3},{8,12},{10,14},{12... | collective-permute-start | bytes 1572872 | tf_op jit(solution)/shard_map/ppermute | solution.py:45
  267.6 40.7 %collective-permute-start.28 = (bf16[128,2048]{1,0:T(8,128)(2,1)}, bf16[128,2048]{1,0:T(8,128)(2,1)}, u32[]{:S(2)}, u32[]{:S(2)}) collective-permute-start(bf16[128,2048]{1,0:T(8,128)(2,1)} %collective-permute-done.24.refs_4_), channel_id=1, source_target_pairs={{0,2},{2,0},{4,6},{6,4},{1,3},{3,1},{5,7},{7,5},{8,10},{10,8},{12,... | collective-permute-start | bytes 1572872 | tf_op jit(solution)/shard_map/ppermute | solution.py:45
  273.1 27.5 %collective-permute-start.58 = (bf16[128,2048]{1,0:T(8,128)(2,1)S(1)}, bf16[128,2048]{1,0:T(8,128)(2,1)S(1)}, u32[]{:S(2)}, u32[]{:S(2)}) collective-permute-start(bf16[128,2048]{1,0:T(8,128)(2,1)S(1)} %collective-permute-done.27.refs_5_), channel_id=1, source_target_pairs={{0,4},{2,6},{4,0},{6,2},{1,5},{3,7},{5,1},{7,3},{8,12},{10,14},{12... | collective-permute-start | bytes 1572872 | tf_op jit(solution)/shard_map/ppermute | solution.py:45
  279.5 32.8 %collective-permute-start.20 = (bf16[128,2048]{1,0:T(8,128)(2,1)}, bf16[128,2048]{1,0:T(8,128)(2,1)}, u32[]{:S(2)}, u32[]{:S(2)}) collective-permute-start(bf16[128,2048]{1,0:T(8,128)(2,1)} %multiply_convert_fusion.refs_0_), channel_id=1, source_target_pairs={{0,2},{2,0},{4,6},{6,4},{1,3},{3,1},{5,7},{7,5},{8,10},{10,8},{12,... | collective-permute-start | bytes 1572872 | tf_op jit(solution)/shard_map/ppermute | solution.py:45
  281.2 31.9 %collective-permute-start.22 = (bf16[128,2048]{1,0:T(8,128)(2,1)}, bf16[128,2048]{1,0:T(8,128)(2,1)}, u32[]{:S(2)}, u32[]{:S(2)}) collective-permute-start(bf16[128,2048]{1,0:T(8,128)(2,1)} %collective-permute-done.21.refs_2_), channel_id=1, source_target_pairs={{0,2},{2,0},{4,6},{6,4},{1,3},{3,1},{5,7},{7,5},{8,10},{10,8},{12,... | collective-permute-start | bytes 1572872 | tf_op jit(solution)/shard_map/ppermute | solution.py:45
  306.0 61.8 %collective-permute-start.59 = (bf16[512,2048]{1,0:T(8,128)(2,1)}, bf16[512,2048]{1,0:T(8,128)(2,1)}, u32[]{:S(2)}, u32[]{:S(2)}) collective-permute-start(bf16[512,2048]{1,0:T(8,128)(2,1)} %get-tuple-element.160), channel_id=1, source_target_pairs={{0,1},{1,0},{2,3},{3,2},{4,5},{5,4},{6,7},{7,6},{8,9},{9,8},{10,11... | collective-permute-start | bytes 6291464 | tf_op jit(solution)/shard_map/ppermute | solution.py:45
  308.3 24.7 %collective-permute-start.30 = (bf16[128,2048]{1,0:T(8,128)(2,1)}, bf16[128,2048]{1,0:T(8,128)(2,1)}, u32[]{:S(2)}, u32[]{:S(2)}) collective-permute-start(bf16[128,2048]{1,0:T(8,128)(2,1)} %collective-permute-done.28.refs_5_), channel_id=1, source_target_pairs={{0,4},{2,6},{4,0},{6,2},{1,5},{3,7},{5,1},{7,3},{8,12},{10,14},{12... | collective-permute-start | bytes 1572872 | tf_op jit(solution)/shard_map/ppermute | solution.py:45
  339.6 54.1 %collective-permute-start.49 = (bf16[512,2048]{1,0:T(8,128)(2,1)}, bf16[512,2048]{1,0:T(8,128)(2,1)}, u32[]{:S(2)}, u32[]{:S(2)}) collective-permute-start(bf16[512,2048]{1,0:T(8,128)(2,1)} %get-tuple-element.137), channel_id=1, source_target_pairs={{0,1},{1,0},{2,3},{3,2},{4,5},{5,4},{6,7},{7,6},{8,9},{9,8},{10,11... | collective-permute-start | bytes 6291464 | tf_op jit(solution)/shard_map/ppermute | solution.py:45
  382.7 42.3 %collective-permute-start.60 = (bf16[512,2048]{1,0:T(8,128)(2,1)}, bf16[512,2048]{1,0:T(8,128)(2,1)}, u32[]{:S(2)}, u32[]{:S(2)}) collective-permute-start(bf16[512,2048]{1,0:T(8,128)(2,1)} %get-tuple-element.161), channel_id=1, source_target_pairs={{0,1},{1,0},{2,3},{3,2},{4,5},{5,4},{6,7},{7,6},{8,9},{9,8},{10,11... | collective-permute-start | bytes 6291464 | tf_op jit(solution)/shard_map/ppermute | solution.py:45
  387.0 132.7 %collective-permute-start.86 = (bf16[512,2048]{1,0:T(8,128)(2,1)}, bf16[512,2048]{1,0:T(8,128)(2,1)}, u32[]{:S(2)}, u32[]{:S(2)}) collective-permute-start(bf16[512,2048]{1,0:T(8,128)(2,1)} %copy-done.44), channel_id=1, source_target_pairs={{0,1},{1,0},{2,3},{3,2},{4,5},{5,4},{6,7},{7,6},{8,9},{9,8},{10,11... | collective-permute-start | bytes 6291464 | tf_op jit(solution)/shard_map/ppermute | solution.py:45
  407.6 48.3 %collective-permute-start.51 = (bf16[512,2048]{1,0:T(8,128)(2,1)}, bf16[512,2048]{1,0:T(8,128)(2,1)}, u32[]{:S(2)}, u32[]{:S(2)}) collective-permute-start(bf16[512,2048]{1,0:T(8,128)(2,1)} %get-tuple-element.138), channel_id=1, source_target_pairs={{0,1},{1,0},{2,3},{3,2},{4,5},{5,4},{6,7},{7,6},{8,9},{9,8},{10,11... | collective-permute-start | bytes 6291464 | tf_op jit(solution)/shard_map/ppermute | solution.py:45
  422.2 31.3 %all-to-all-start.1 = ((f32[32,1,64]{2,1,0:T(1,128)}), f32[32,1,64]{2,1,0:T(1,128)S(1)}, u32[]{:S(2)}, u32[]{:S(2)}) async-start(f32[32,1,64]{2,1,0:T(1,128)} %bitcast.66), calls=%async_computation.1 | async-start | bytes 32768 | tf_op jit(solution)/shard_map/all_to_all | solution.py:773
  434.0 28.3 %collective-permute-start.64 = (bf16[128,2048]{1,0:T(8,128)(2,1)}, bf16[128,2048]{1,0:T(8,128)(2,1)}, u32[]{:S(2)}, u32[]{:S(2)}) collective-permute-start(bf16[128,2048]{1,0:T(8,128)(2,1)} %get-tuple-element.168), channel_id=1, source_target_pairs={{0,4},{2,6},{4,0},{6,2},{1,5},{3,7},{5,1},{7,3},{8,12},{10,14},{12... | collective-permute-start | bytes 1572872 | tf_op jit(solution)/shard_map/ppermute | solution.py:45
  455.4 25.5 %collective-permute-start.66 = (bf16[128,2048]{1,0:T(8,128)(2,1)}, bf16[128,2048]{1,0:T(8,128)(2,1)S(1)}, u32[]{:S(2)}, u32[]{:S(2)}) collective-permute-start(bf16[128,2048]{1,0:T(8,128)(2,1)} %get-tuple-element.169), channel_id=1, source_target_pairs={{0,4},{2,6},{4,0},{6,2},{1,5},{3,7},{5,1},{7,3},{8,12},{10,14},{12... | collective-permute-start | bytes 1572872 | tf_op jit(solution)/shard_map/ppermute | solution.py:45
  461.9 31.2 %collective-permute-start.53 = (bf16[128,2048]{1,0:T(8,128)(2,1)S(1)}, bf16[128,2048]{1,0:T(8,128)(2,1)S(1)}, u32[]{:S(2)}, u32[]{:S(2)}) collective-permute-start(bf16[128,2048]{1,0:T(8,128)(2,1)S(1)} %get-tuple-element.149), channel_id=1, source_target_pairs={{0,2},{2,0},{4,6},{6,4},{1,3},{3,1},{5,7},{7,5},{8,10},{10,8},{12,... | collective-permute-start | bytes 1572872 | tf_op jit(solution)/shard_map/ppermute | solution.py:45
  481.0 33.5 %collective-permute-start.61 = (bf16[128,2048]{1,0:T(8,128)(2,1)S(1)}, bf16[128,2048]{1,0:T(8,128)(2,1)S(1)}, u32[]{:S(2)}, u32[]{:S(2)}) collective-permute-start(bf16[128,2048]{1,0:T(8,128)(2,1)S(1)} %copy-done.52), channel_id=1, source_target_pairs={{0,2},{2,0},{4,6},{6,4},{1,3},{3,1},{5,7},{7,5},{8,10},{10,8},{12,... | collective-permute-start | bytes 1572872 | tf_op jit(solution)/shard_map/ppermute | solution.py:45
  519.8 84.9 %collective-permute-start.50 = (bf16[512,2048]{1,0:T(8,128)(2,1)}, bf16[512,2048]{1,0:T(8,128)(2,1)}, u32[]{:S(2)}, u32[]{:S(2)}) collective-permute-start(bf16[512,2048]{1,0:T(8,128)(2,1)} %get-tuple-element.143), channel_id=1, source_target_pairs={{0,1},{1,0},{2,3},{3,2},{4,5},{5,4},{6,7},{7,6},{8,9},{9,8},{10,11... | collective-permute-start | bytes 6291464 | tf_op jit(solution)/shard_map/ppermute | solution.py:45
  528.2 37.9 %collective-permute-start.90 = (bf16[128,2048]{1,0:T(8,128)(2,1)}, bf16[128,2048]{1,0:T(8,128)(2,1)}, u32[]{:S(2)}, u32[]{:S(2)}) collective-permute-start(bf16[128,2048]{1,0:T(8,128)(2,1)} %get-tuple-element.198), channel_id=1, source_target_pairs={{0,4},{2,6},{4,0},{6,2},{1,5},{3,7},{5,1},{7,3},{8,12},{10,14},{12... | collective-permute-start | bytes 1572872 | tf_op jit(solution)/shard_map/ppermute | solution.py:45
  560.5 51.3 %collective-permute-start.87 = (bf16[128,2048]{1,0:T(8,128)(2,1)}, bf16[128,2048]{1,0:T(8,128)(2,1)S(1)}, u32[]{:S(2)}, u32[]{:S(2)}) collective-permute-start(bf16[128,2048]{1,0:T(8,128)(2,1)} %get-tuple-element.193), channel_id=1, source_target_pairs={{0,2},{2,0},{4,6},{6,4},{1,3},{3,1},{5,7},{7,5},{8,10},{10,8},{12,... | collective-permute-start | bytes 1572872 | tf_op jit(solution)/shard_map/ppermute | solution.py:45
  562.0 31.1 %collective-permute-start.88 = (bf16[128,2048]{1,0:T(8,128)(2,1)}, bf16[128,2048]{1,0:T(8,128)(2,1)S(1)}, u32[]{:S(2)}, u32[]{:S(2)}) collective-permute-start(bf16[128,2048]{1,0:T(8,128)(2,1)} %get-tuple-element.195), channel_id=1, source_target_pairs={{0,2},{2,0},{4,6},{6,4},{1,3},{3,1},{5,7},{7,5},{8,10},{10,8},{12,... | collective-permute-start | bytes 1572872 | tf_op jit(solution)/shard_map/ppermute | solution.py:45
  563.6 24.8 %collective-permute-start.75 = (bf16[64,2048]{1,0:T(8,128)(2,1)S(1)}, bf16[64,2048]{1,0:T(8,128)(2,1)S(1)}, u32[]{:S(2)}, u32[]{:S(2)}) collective-permute-start(bf16[64,2048]{1,0:T(8,128)(2,1)S(1)} %slice.416), channel_id=1, source_target_pairs={{0,2},{2,0},{4,6},{6,4},{1,3},{3,1},{5,7},{7,5},{8,10},{10,8},{12,... | collective-permute-start | bytes 786440 | tf_op jit(solution)/shard_map/ppermute | solution.py:45
  566.1 24.9 %collective-permute-start.76 = (bf16[64,2048]{1,0:T(8,128)(2,1)S(1)}, bf16[64,2048]{1,0:T(8,128)(2,1)S(1)}, u32[]{:S(2)}, u32[]{:S(2)}) collective-permute-start(bf16[64,2048]{1,0:T(8,128)(2,1)S(1)} %slice.417), channel_id=1, source_target_pairs={{0,4},{2,6},{4,0},{6,2},{1,5},{3,7},{5,1},{7,3},{8,12},{10,14},{12... | collective-permute-start | bytes 786440 | tf_op jit(solution)/shard_map/ppermute | solution.py:45
  651.7 25.5 %collective-permute-start.109 = (bf16[512,512]{1,0:T(8,128)(2,1)S(1)}, bf16[512,512]{1,0:T(8,128)(2,1)S(1)}, u32[]{:S(2)}, u32[]{:S(2)}) collective-permute-start(bf16[512,512]{1,0:T(8,128)(2,1)S(1)} %get-tuple-element.308), channel_id=1, source_target_pairs={{0,6},{2,4},{4,2},{6,0},{1,7},{3,5},{5,3},{7,1},{8,14},{10,12},{12... | collective-permute-start | bytes 1572872 | tf_op jit(solution)/shard_map/ppermute | solution.py:45
  653.1 37.0 %collective-permute-start.103 = (bf16[512,512]{1,0:T(8,128)(2,1)S(1)}, bf16[512,512]{1,0:T(8,128)(2,1)S(1)}, u32[]{:S(2)}, u32[]{:S(2)}) collective-permute-start(bf16[512,512]{1,0:T(8,128)(2,1)S(1)} %get-tuple-element.309), channel_id=1, source_target_pairs={{0,4},{2,6},{4,0},{6,2},{1,5},{3,7},{5,1},{7,3},{8,12},{10,14},{12... | collective-permute-start | bytes 1572872 | tf_op jit(solution)/shard_map/ppermute | solution.py:45
  655.2 36.7 %collective-permute-start.122 = (bf16[512,512]{1,0:T(8,128)(2,1)S(1)}, bf16[512,512]{1,0:T(8,128)(2,1)S(1)}, u32[]{:S(2)}, u32[]{:S(2)}) collective-permute-start(bf16[512,512]{1,0:T(8,128)(2,1)S(1)} %get-tuple-element.307), channel_id=1, source_target_pairs={{0,8},{24,16},{1,9},{25,17},{2,10},{26,18},{3,11},{27,19},{4,12},{... | collective-permute-start | bytes 1572872 | tf_op jit(solution)/shard_map/ppermute | solution.py:511
  660.2 35.2 %collective-permute-start.114 = (bf16[512,768]{1,0:T(8,128)(2,1)S(1)}, bf16[512,768]{1,0:T(8,128)(2,1)S(1)}, u32[]{:S(2)}, u32[]{:S(2)}) collective-permute-start(bf16[512,768]{1,0:T(8,128)(2,1)S(1)} %get-tuple-element.302), channel_id=1, source_target_pairs={{0,6},{2,4},{4,2},{6,0},{1,7},{3,5},{5,3},{7,1},{8,14},{10,12},{12... | collective-permute-start | bytes 2359304 | tf_op jit(solution)/shard_map/ppermute | solution.py:45
  666.5 37.2 %collective-permute-start.108 = (bf16[512,768]{1,0:T(8,128)(2,1)S(1)}, bf16[512,768]{1,0:T(8,128)(2,1)S(1)}, u32[]{:S(2)}, u32[]{:S(2)}) collective-permute-start(bf16[512,768]{1,0:T(8,128)(2,1)S(1)} %get-tuple-element.303), channel_id=1, source_target_pairs={{0,4},{2,6},{4,0},{6,2},{1,5},{3,7},{5,1},{7,3},{8,12},{10,14},{12... | collective-permute-start | bytes 2359304 | tf_op jit(solution)/shard_map/ppermute | solution.py:45
  695.4 221.1 %collective-permute-start.94 = (bf16[128,2048]{1,0:T(8,128)(2,1)}, bf16[128,2048]{1,0:T(8,128)(2,1)}, u32[]{:S(2)}, u32[]{:S(2)}) collective-permute-start(bf16[128,2048]{1,0:T(8,128)(2,1)} %add_convert_fusion.22), channel_id=1, source_target_pairs={{0,16},{8,24},{16,0},{24,8},{1,17},{9,25},{17,1},{25,9},{2,18},{10... | collective-permute-start | bytes 1572872 | tf_op jit(solution)/shard_map/ppermute | solution.py:45
  703.7 110.2 %collective-permute-start.78 = (bf16[4,128,2048]{2,1,0:T(8,128)(2,1)S(1)}, bf16[4,128,2048]{2,1,0:T(8,128)(2,1)S(1)}, u32[]{:S(2)}, u32[]{:S(2)}) collective-permute-start(bf16[4,128,2048]{2,1,0:T(8,128)(2,1)S(1)} %bitcast.251), channel_id=1, source_target_pairs={{0,1},{1,0},{2,3},{3,2},{4,5},{5,4},{6,7},{7,6},{8,9},{9,8},{10,11... | collective-permute-start | bytes 6291464 | tf_op jit(solution)/shard_map/ppermute | solution.py:45
  707.7 55.3 %collective-permute-start.129 = (bf16[512,512]{1,0:T(8,128)(2,1)S(1)}, bf16[512,512]{1,0:T(8,128)(2,1)S(1)}, u32[]{:S(2)}, u32[]{:S(2)}) collective-permute-start(bf16[512,512]{1,0:T(8,128)(2,1)S(1)} %add_convert_fusion.16), channel_id=1, source_target_pairs={{8,16},{16,8},{9,17},{17,9},{10,18},{18,10},{11,19},{19,11},{12,20... | collective-permute-start | bytes 1572872 | tf_op jit(solution)/shard_map/ppermute | solution.py:513
  710.0 88.8 %collective-permute-start.101 = (bf16[512,512]{1,0:T(8,128)(2,1)S(1)}, bf16[512,512]{1,0:T(8,128)(2,1)S(1)}, u32[]{:S(2)}, u32[]{:S(2)}) collective-permute-start(bf16[512,512]{1,0:T(8,128)(2,1)S(1)} %add_convert_fusion.17), channel_id=1, source_target_pairs={{8,0},{16,24},{9,1},{17,25},{10,2},{18,26},{11,3},{19,27},{12,4},{... | collective-permute-start | bytes 1572872 | tf_op jit(solution)/shard_map/ppermute | solution.py:514
  711.4 63.4 %collective-permute-start.115 = (bf16[512,512]{1,0:T(8,128)(2,1)S(1)}, bf16[512,512]{1,0:T(8,128)(2,1)S(1)}, u32[]{:S(2)}, u32[]{:S(2)}) collective-permute-start(bf16[512,512]{1,0:T(8,128)(2,1)S(1)} %slice.359), channel_id=1, source_target_pairs={{0,8},{24,16},{1,9},{25,17},{2,10},{26,18},{3,11},{27,19},{4,12},{... | collective-permute-start | bytes 1572872 | tf_op jit(solution)/shard_map/ppermute | solution.py:511
  797.2 52.1 %collective-permute-start.128 = (bf16[512,512]{1,0:T(8,128)(2,1)S(1)}, bf16[512,512]{1,0:T(8,128)(2,1)S(1)}, u32[]{:S(2)}, u32[]{:S(2)}) collective-permute-start(bf16[512,512]{1,0:T(8,128)(2,1)S(1)} %add_convert_fusion.2), channel_id=1, source_target_pairs={{8,0},{16,24},{9,1},{17,25},{10,2},{18,26},{11,3},{19,27},{12,4},{... | collective-permute-start | bytes 1572872 | tf_op jit(solution)/shard_map/ppermute | solution.py:514
  798.8 58.6 %collective-permute-start.132 = (bf16[512,512]{1,0:T(8,128)(2,1)S(1)}, bf16[512,512]{1,0:T(8,128)(2,1)S(1)}, u32[]{:S(2)}, u32[]{:S(2)}) collective-permute-start(bf16[512,512]{1,0:T(8,128)(2,1)S(1)} %add_convert_fusion), channel_id=1, source_target_pairs={{8,0},{16,24},{9,1},{17,25},{10,2},{18,26},{11,3},{19,27},{12,4},{... | collective-permute-start | bytes 1572872 | tf_op jit(solution)/shard_map/ppermute | solution.py:514
  815.4 26.7 %collective-permute-start.106 = (bf16[512,512]{1,0:T(8,128)(2,1)S(1)}, bf16[512,512]{1,0:T(8,128)(2,1)S(1)}, u32[]{:S(2)}, u32[]{:S(2)}) collective-permute-start(bf16[512,512]{1,0:T(8,128)(2,1)S(1)} %add_convert_fusion.15), channel_id=1, source_target_pairs={{8,16},{16,8},{9,17},{17,9},{10,18},{18,10},{11,19},{19,11},{12,20... | collective-permute-start | bytes 1572872 | tf_op jit(solution)/shard_map/ppermute | solution.py:513
  816.2 32.3 %collective-permute-start.119 = (bf16[512,512]{1,0:T(8,128)(2,1)S(1)}, bf16[512,512]{1,0:T(8,128)(2,1)S(1)}, u32[]{:S(2)}, u32[]{:S(2)}) collective-permute-start(bf16[512,512]{1,0:T(8,128)(2,1)S(1)} %add_convert_fusion.8), channel_id=1, source_target_pairs={{0,8},{24,16},{1,9},{25,17},{2,10},{26,18},{3,11},{27,19},{4,12},{... | collective-permute-start | bytes 1572872 | tf_op jit(solution)/shard_map/ppermute | solution.py:511
  855.9 36.8 %collective-permute-start.117 = (bf16[512,512]{1,0:T(8,128)(2,1)S(1)}, bf16[512,512]{1,0:T(8,128)(2,1)S(1)}, u32[]{:S(2)}, u32[]{:S(2)}) collective-permute-start(bf16[512,512]{1,0:T(8,128)(2,1)S(1)} %add_convert_fusion.9), channel_id=1, source_target_pairs={{8,0},{16,24},{9,1},{17,25},{10,2},{18,26},{11,3},{19,27},{12,4},{... | collective-permute-start | bytes 1572872 | tf_op jit(solution)/shard_map/ppermute | solution.py:514
  857.4 33.8 %collective-permute-start.113 = (bf16[512,512]{1,0:T(8,128)(2,1)S(1)}, bf16[512,512]{1,0:T(8,128)(2,1)S(1)}, u32[]{:S(2)}, u32[]{:S(2)}) collective-permute-start(bf16[512,512]{1,0:T(8,128)(2,1)S(1)} %add_convert_fusion.11), channel_id=1, source_target_pairs={{8,0},{16,24},{9,1},{17,25},{10,2},{18,26},{11,3},{19,27},{12,4},{... | collective-permute-start | bytes 1572872 | tf_op jit(solution)/shard_map/ppermute | solution.py:514
  858.8 29.2 %collective-permute-start.107 = (bf16[512,512]{1,0:T(8,128)(2,1)S(1)}, bf16[512,512]{1,0:T(8,128)(2,1)S(1)}, u32[]{:S(2)}, u32[]{:S(2)}) collective-permute-start(bf16[512,512]{1,0:T(8,128)(2,1)S(1)} %add_convert_fusion.14), channel_id=1, source_target_pairs={{8,0},{16,24},{9,1},{17,25},{10,2},{18,26},{11,3},{19,27},{12,4},{... | collective-permute-start | bytes 1572872 | tf_op jit(solution)/shard_map/ppermute | solution.py:514
  861.1 31.9 %collective-permute-start.82 = (bf16[128,2048]{1,0:T(8,128)(2,1)S(1)}, bf16[128,2048]{1,0:T(8,128)(2,1)S(1)}, u32[]{:S(2)}, u32[]{:S(2)}) collective-permute-start(bf16[128,2048]{1,0:T(8,128)(2,1)S(1)} %pad_maximum_fusion.14), channel_id=1, source_target_pairs={{0,4},{2,6},{4,0},{6,2},{1,5},{3,7},{5,1},{7,3},{8,12},{10,14},{12... | collective-permute-start | bytes 1572872 | tf_op jit(solution)/shard_map/ppermute | solution.py:45
  891.1 52.0 %collective-permute-start.121 = (bf16[512,512]{1,0:T(8,128)(2,1)}, bf16[512,512]{1,0:T(8,128)(2,1)}, u32[]{:S(2)}, u32[]{:S(2)}) collective-permute-start(bf16[512,512]{1,0:T(8,128)(2,1)} %add_convert_fusion.6), channel_id=1, source_target_pairs={{8,0},{16,24},{9,1},{17,25},{10,2},{18,26},{11,3},{19,27},{12,4},{... | collective-permute-start | bytes 1572872 | tf_op jit(solution)/shard_map/ppermute | solution.py:514
  916.5 49.7 %collective-permute-start.83 = (bf16[128,2048]{1,0:T(8,128)(2,1)S(1)}, bf16[128,2048]{1,0:T(8,128)(2,1)}, u32[]{:S(2)}, u32[]{:S(2)}) collective-permute-start(bf16[128,2048]{1,0:T(8,128)(2,1)S(1)} %copy-done.48), channel_id=1, source_target_pairs={{0,2},{2,0},{4,6},{6,4},{1,3},{3,1},{5,7},{7,5},{8,10},{10,8},{12,... | collective-permute-start | bytes 1572872 | tf_op jit(solution)/shard_map/ppermute | solution.py:45
  929.4 36.9 %collective-permute-start.85 = (bf16[128,2048]{1,0:T(8,128)(2,1)}, bf16[128,2048]{1,0:T(8,128)(2,1)}, u32[]{:S(2)}, u32[]{:S(2)}) collective-permute-start(bf16[128,2048]{1,0:T(8,128)(2,1)} %add_convert_fusion.26), channel_id=1, source_target_pairs={{0,4},{2,6},{4,0},{6,2},{1,5},{3,7},{5,1},{7,3},{8,12},{10,14},{12... | collective-permute-start | bytes 1572872 | tf_op jit(solution)/shard_map/ppermute | solution.py:45
  (192 other events, 2297.2 us)
